TPU v7x, 32 devices: a whole 2x2x4 slice. The times are simulated.
32 devices in a mesh: replica: 8 (over y, x, core), fsdp: 4 (over z).
Axes of the slice: x: 2, y: 2, z: 4, core: 2. Of those that a mesh axis runs over, the one named last changes fastest.
Arguments:
- momentum: bfloat16 [8, 4, 384, 1024], P('replica', None, 'fsdp'), may hold values from -400 to 400
- weights: bfloat16 [8, 4, 384, 1024], P('replica', 'fsdp'), may hold values from -6 to 6
- tokens: bfloat16 [8, 1024, 1024], P('replica', 'fsdp'), may hold values from -6 to 6
- routes: int32 [8, 1024, 1], P('replica', 'fsdp'), may hold values from 0 to 3; in each aligned block of 256 rows (0 to 255, 256 to 511, ..., all dimensions but the last counted through in order) at most 128 rows name the same one
Outputs:
- new_weight: bfloat16 [8, 4, 384, 1024], P('replica', 'fsdp')
- expert_rows: bfloat16 [8, 4, 512, 384], P('replica', 'fsdp')
Inputs may be any that keep to these rules, and one draw needn't show every extreme that they name: `routes`: within one replica, the 256 rows of one device name each expert at most 128 times, a bound that some block reaches.
All inputs are finite; a program needn't handle non-finite values.
Results may differ from a plain program's by a relative error of at most 0.008.
Values may be sent and summed in bfloat16 or wider, within the bound.
No kernel may reach another device: no remote copies, remote signals or barrier semaphores. Data moves between devices by JAX's collectives and lax.ppermute only.
A program may use at most 64 MiB of HBM per device.

v0:
```python
import functools
import math

import jax
import jax.numpy as jnp
from jax import lax
from jax.experimental import pallas as pl
from jax.experimental.pallas import tpu as pltpu
from jax.sharding import PartitionSpec as P


ITERS = 2
GOSSIP_BIT = 2


coef_a = 3.4445
coef_b = -4.775
coef_c = 2.0315
step_rate = 0.5

VMEM = pl.BlockSpec(memory_space=pltpu.VMEM)
SMEM = pl.BlockSpec(memory_space=pltpu.SMEM)


def dot(a, b):
    return jnp.dot(a, b, preferred_element_type=jnp.float32)


def dot_t(a, b):
    return lax.dot_general(a, b, (((1,), (1,)), ((), ())), preferred_element_type=jnp.float32)


def other(me, hop, nodes):
    if nodes & (nodes - 1) == 0:
        return me ^ hop
    return lax.rem(hop - me + nodes, nodes)


def far_first(nodes):
    return (*range(2, nodes), 1) if nodes > 1 else ()


def trade(block, hop, nodes):
    if nodes & (nodes - 1) == 0:
        pairs = [(i, i ^ hop) for i in range(nodes)]
    else:
        pairs = [(i, (hop - i) % nodes) for i in range(nodes)]
    return lax.ppermute(block, "fsdp", pairs)


def pack_kernel(nodes, capacity, place_ref, routes_ref, tokens_ref, *out_refs):
    tok_rows = routes_ref.shape[1]
    routes = routes_ref[...]
    earlier = lax.broadcasted_iota(jnp.int32, (tok_rows, tok_rows), 0) < lax.broadcasted_iota(
        jnp.int32, (tok_rows, tok_rows), 1
    )
    earlier = jnp.where(earlier, 1.0, 0.0).astype(jnp.bfloat16)
    slot = lax.broadcasted_iota(jnp.int32, (capacity, tok_rows), 0)
    tokens = tokens_ref[...]
    for k in range(nodes):
        here = routes == place_ref[k]
        count = dot(jnp.where(here, 1.0, 0.0).astype(jnp.bfloat16), earlier)
        position = jnp.where(here, count.astype(jnp.int32), -1)
        placing = jnp.where(slot == position, 1.0, 0.0).astype(jnp.bfloat16)
        out_refs[k][...] = dot(placing, tokens).astype(jnp.bfloat16)


def update_kernel(nodes, width, place_ref, *refs):
    blocks, weight_ref, out_ref, x_ref = refs[:nodes], refs[nodes], refs[nodes + 1], refs[nodes + 2]
    rows = blocks[0].shape[0]
    total = nodes * rows
    for k in range(nodes):
        x_ref[k * rows : (k + 1) * rows, :] = blocks[k][...]
    x = x_ref[...]
    gram = dot_t(x, x)
    on_diagonal = lax.broadcasted_iota(jnp.int32, (total, total), 0) == lax.broadcasted_iota(
        jnp.int32, (total, total), 1
    )
    square = jnp.sum(jnp.where(on_diagonal, gram, 0.0))
    scale = 1.0 / (jnp.sqrt(jnp.full((1, 1), square, jnp.float32)) + 1e-07)
    gram = gram * scale * scale
    keep, mix = 1.0, None
    now = gram
    for step in range(ITERS):
        low = now.astype(jnp.bfloat16)
        poly = coef_b * now + coef_c * dot(low, low)
        poly_low = poly.astype(jnp.bfloat16)
        if step + 1 < ITERS:
            first = dot(poly_low, low)
            second = dot(poly_low, first.astype(jnp.bfloat16))
            now = coef_a * coef_a * now + 2.0 * coef_a * first + second
        if mix is None:
            mix = keep * poly
        else:
            mix = coef_a * mix + keep * poly + dot(poly_low, mix.astype(jnp.bfloat16))
        keep = keep * coef_a
    mix = (mix * scale).astype(jnp.bfloat16)
    rate = step_rate * math.sqrt(width)
    for k in range(nodes):
        change = dot(mix[k * rows : (k + 1) * rows, :], x) + (keep * scale) * blocks[k][...].astype(
            jnp.float32
        )
        at = pl.ds(pl.multiple_of(place_ref[k] * rows, rows), rows)
        out_ref[at, :] = (weight_ref[at, :].astype(jnp.float32) - rate * change).astype(jnp.bfloat16)


def project_kernel(nodes, width, place_ref, *refs):
    blocks, own_ref, partner_ref = refs[:nodes], refs[nodes], refs[nodes + 1]
    weight_ref, rows_ref, slot_ref = refs[nodes + 2], refs[nodes + 3], refs[nodes + 4]
    capacity = blocks[0].shape[0]
    weight = (
        0.5 * (own_ref[...].astype(jnp.float32) + partner_ref[...].astype(jnp.float32))
    ).astype(jnp.bfloat16)
    weight_ref[...] = weight
    for k in range(nodes):
        at = pl.ds(pl.multiple_of(place_ref[k] * capacity, capacity), capacity)
        slot_ref[at, :] = blocks[k][...]
    rows_ref[...] = (dot_t(slot_ref[...], weight) * (1.0 / math.sqrt(width))).astype(jnp.bfloat16)


def per_device(momentum, weights, tokens, routes):
    nodes = lax.axis_size("fsdp")
    me = lax.axis_index("fsdp")
    width = momentum.shape[3]
    total = weights.shape[2]
    tok_rows = tokens.shape[1]
    capacity = 2 * tok_rows // nodes
    hops = range(1, nodes)
    place = jnp.stack([other(me, k, nodes) for k in range(nodes)]).astype(jnp.int32)

    shards = [lax.dynamic_index_in_dim(momentum[0], place[k], 0, False) for k in range(nodes)]
    blocks = {0: shards[0]}
    for k in far_first(nodes):
        blocks[k] = trade(shards[k], k, nodes)

    packed = list(
        pl.pallas_call(
            functools.partial(pack_kernel, nodes, capacity),
            out_shape=[jax.ShapeDtypeStruct((capacity, width), jnp.bfloat16)] * nodes,
            in_specs=[SMEM, VMEM, VMEM],
            out_specs=[VMEM] * nodes,
            compiler_params=pltpu.CompilerParams(vmem_limit_bytes=16 << 20),
            cost_estimate=pl.CostEstimate(
                flops=2 * nodes * capacity * tok_rows * width,
                bytes_accessed=2 * (tok_rows + nodes * capacity) * width,
                transcendentals=0,
            ),
            name="pack",
        )(place, routes.reshape(1, tok_rows), tokens[0])
    )
    slots = {0: packed[0]}
    for k in hops:
        slots[k] = trade(packed[k], k, nodes)
    blocks = [blocks[k] for k in range(nodes)]
    slots = [slots[k] for k in range(nodes)]

    updated = pl.pallas_call(
        functools.partial(update_kernel, nodes, width),
        out_shape=jax.ShapeDtypeStruct((total, width), jnp.bfloat16),
        in_specs=[SMEM] + [VMEM] * (nodes + 1),
        out_specs=VMEM,
        scratch_shapes=[pltpu.VMEM((total, width), jnp.bfloat16)],
        compiler_params=pltpu.CompilerParams(vmem_limit_bytes=24 << 20),
        cost_estimate=pl.CostEstimate(
            flops=4 * total * total * width + 10 * total**3,
            bytes_accessed=6 * total * width,
            transcendentals=0,
        ),
        name="update",
    )(place, *blocks, weights[0, 0])
    partner = lax.ppermute(
        updated, "replica", [(i, i ^ 1 << GOSSIP_BIT) for i in range(lax.axis_size("replica"))]
    )
    averaged, expert_rows = pl.pallas_call(
        functools.partial(project_kernel, nodes, width),
        out_shape=(
            jax.ShapeDtypeStruct((total, width), jnp.bfloat16),
            jax.ShapeDtypeStruct((nodes * capacity, total), jnp.bfloat16),
        ),
        in_specs=[SMEM] + [VMEM] * (nodes + 2),
        out_specs=(VMEM, VMEM),
        scratch_shapes=[pltpu.VMEM((nodes * capacity, width), jnp.bfloat16)],
        compiler_params=pltpu.CompilerParams(vmem_limit_bytes=24 << 20),
        cost_estimate=pl.CostEstimate(
            flops=2 * nodes * capacity * width * total,
            bytes_accessed=6 * total * width + 2 * nodes * capacity * (width + total),
            transcendentals=0,
        ),
        name="project",
    )(place, *slots, updated, partner)
    return (averaged[None, None], expert_rows[None, None])


def solution(mesh):
    in_specs = (
        P("replica", None, "fsdp", None),
        P("replica", "fsdp", None, None),
        P("replica", "fsdp", None),
        P("replica", "fsdp", None),
    )
    out_specs = (P("replica", "fsdp", None, None), P("replica", "fsdp", None, None))

    return jax.shard_map(per_device, mesh=mesh, in_specs=in_specs, out_specs=out_specs, check_vma=False)
```

profile of v0, /device:TPU:8, one launch (start us, length us, event | category | flops | bytes accessed | tf_op | source)
XLA Modules:
  0.0 55.8 jit_solution(17578489096858810010)
XLA Ops:
  0.7 0.0 copy-start
  0.7 1.3 %dynamic-slice_bitcast_fusion = (bf16[96,1024]{1,0:T(8,128)(2,1)S(1)}, bf16[96,1024]{1,0:T(8,128)(2,1)S(1)}, bf16[96,1024]{1,0:T(8,128)(2,1)S(1)}, bf16[96,1024]{1,0:T(8,128)(2,1)S(1)}) fusion(bf16[1,4,96,1024]{3,2,1,0:T(8,128)(2,1)} %param.4, s32[]{:T(128)S(6)} %select_n.16, s32[]{:T(128)S(6)} %select_n.14, s32[]{:T(128)S(6)} %select_n.13, s32[]{:T(128)S(6)} %select_n.15), kind=kLoop, calls=%fused_computation | loop fusion | bytes 1572880 | tf_op jit(solution)/shard_map/jit(dynamic_index_in_dim)/squeeze | solution.py:131
  2.0 1.6 %collective-permute-start.5 = (bf16[96,1024]{1,0:T(8,128)(2,1)S(1)}, bf16[96,1024]{1,0:T(8,128)(2,1)S(1)}, u32[]{:S(2)}, u32[]{:S(2)}) collective-permute-start(bf16[96,1024]{1,0:T(8,128)(2,1)S(1)} %get-tuple-element.14), channel_id=1, source_target_pairs={{0,3},{1,2},{2,1},{3,0},{4,7},{5,6},{6,5},{7,4},{8,11},{9,10},{10,... | collective-permute-start | bytes 589832 | tf_op jit(solution)/shard_map/ppermute | solution.py:48
  3.6 2.5 %collective-permute-start.3 = (bf16[96,1024]{1,0:T(8,128)(2,1)S(1)}, bf16[96,1024]{1,0:T(8,128)(2,1)S(1)}, u32[]{:S(2)}, u32[]{:S(2)}) collective-permute-start(bf16[96,1024]{1,0:T(8,128)(2,1)S(1)} %get-tuple-element.15), channel_id=1, source_target_pairs={{0,1},{1,0},{2,3},{3,2},{4,5},{5,4},{6,7},{7,6},{8,9},{9,8},{10,11... | collective-permute-start | bytes 589832 | tf_op jit(solution)/shard_map/ppermute | solution.py:48
  6.1 0.0 collective-permute-start.4
  6.1 0.1 pad_add_fusion.place_ref
  6.2 8.5 %collective-permute-done.5.refs_3_ = bf16[96,1024]{1,0:T(8,128)(2,1)S(1)} collective-permute-done((bf16[96,1024]{1,0:T(8,128)(2,1)S(1)}, bf16[96,1024]{1,0:T(8,128)(2,1)S(1)}, u32[]{:S(2)}, u32[]{:S(2)}) %collective-permute-start.5) | collective-permute-done | bytes 196640 | tf_op jit(solution)/shard_map/ppermute | solution.py:48
  14.7 1.4 %collective-permute-done.3.refs_1_ = bf16[96,1024]{1,0:T(8,128)(2,1)S(1)} collective-permute-done((bf16[96,1024]{1,0:T(8,128)(2,1)S(1)}, bf16[96,1024]{1,0:T(8,128)(2,1)S(1)}, u32[]{:S(2)}, u32[]{:S(2)}) %collective-permute-start.3) | collective-permute-done | bytes 196640 | tf_op jit(solution)/shard_map/ppermute | solution.py:48
  16.1 4.4 %collective-permute-done.4.refs_2_ = bf16[96,1024]{1,0:T(8,128)(2,1)S(1)} collective-permute-done((bf16[96,1024]{1,0:T(8,128)(2,1)S(1)}, bf16[96,1024]{1,0:T(8,128)(2,1)S(1)}, u32[]{:S(2)}, u32[]{:S(2)}) %collective-permute-start.4) | collective-permute-done | bytes 196640 | tf_op jit(solution)/shard_map/ppermute | solution.py:48
  20.4 0.0 copy-done
  20.5 0.0 copy-start.1
  20.5 3.5 %update.1.refs_4_ = bf16[384,1024]{1,0:T(8,128)(2,1)S(1)} custom-call(s32[4]{0:T(128)S(1)} %pad_add_fusion.place_ref, bf16[96,1024]{1,0:T(8,128)(2,1)S(1)} %get-tuple-element.16.refs_0_, bf16[96,1024]{1,0:T(8,128)(2,1)S(1)} %collective-permute-done.3.refs_1_, bf16[96,1024]{1,0:T(8,128)(2,1)S(1)} %collective-permute-done.4.refs_2_, ...), custom_call_target="tpu_custom_call" | custom-call | flops 1170210816 | bytes 2359296 | tf_op jit(solution)/shard_map/update/pallas_call | solution.py:157
  23.9 1.6 %collective-permute-start.6 = (bf16[384,1024]{1,0:T(8,128)(2,1)S(1)}, bf16[384,1024]{1,0:T(8,128)(2,1)S(1)}, u32[]{:S(2)}, u32[]{:S(2)}) collective-permute-start(bf16[384,1024]{1,0:T(8,128)(2,1)S(1)} %update.1.refs_4_), channel_id=1, source_target_pairs={{0,16},{4,20},{8,24},{12,28},{16,0},{20,4},{24,8},{28,12},{1,17},{... | collective-permute-start | bytes 2359304 | tf_op jit(solution)/shard_map/ppermute | solution.py:171
  25.5 0.0 copy-done.1
  25.5 0.7 %copy-done.2 = s32[1,256,1]{1,2,0:T(1,128)S(1)} copy-done((s32[1,256,1]{1,2,0:T(1,128)S(1)}, s32[1,256,1]{1,2,0:T(1,128)}, u32[]{:S(2)}) %copy-start.2) | copy-done | bytes 1048
  26.2 1.5 %pack.1 = (bf16[128,1024]{1,0:T(8,128)(2,1)S(1)}, bf16[128,1024]{1,0:T(8,128)(2,1)S(1)}, bf16[128,1024]{1,0:T(8,128)(2,1)S(1)}, bf16[128,1024]{1,0:T(8,128)(2,1)S(1)}) custom-call(s32[4]{0:T(128)S(1)} %pad_add_fusion.place_ref, s32[1,256]{1,0:T(1,128)S(1)} %bitcast.19, bf16[256,1024]{1,0:T(8,128)(2,1)S(1)} %bitcast.18), custom_call_target="tpu_custom_call" | custom-call | flops 268435456 | bytes 1572864 | tf_op jit(solution)/shard_map/pack/pallas_call | solution.py:137
  27.8 2.4 %collective-permute-start = (bf16[128,1024]{1,0:T(8,128)(2,1)S(1)}, bf16[128,1024]{1,0:T(8,128)(2,1)S(1)}, u32[]{:S(2)}, u32[]{:S(2)}) collective-permute-start(bf16[128,1024]{1,0:T(8,128)(2,1)S(1)} %get-tuple-element.9), channel_id=1, source_target_pairs={{0,1},{1,0},{2,3},{3,2},{4,5},{5,4},{6,7},{7,6},{8,9},{9,8},{10,11... | collective-permute-start | bytes 786440 | tf_op jit(solution)/shard_map/ppermute | solution.py:48
  30.2 1.1 %collective-permute-start.1 = (bf16[128,1024]{1,0:T(8,128)(2,1)S(1)}, bf16[128,1024]{1,0:T(8,128)(2,1)S(1)}, u32[]{:S(2)}, u32[]{:S(2)}) collective-permute-start(bf16[128,1024]{1,0:T(8,128)(2,1)S(1)} %get-tuple-element.10), channel_id=1, source_target_pairs={{0,2},{1,3},{2,0},{3,1},{4,6},{5,7},{6,4},{7,5},{8,10},{9,11},{10,... | collective-permute-start | bytes 786440 | tf_op jit(solution)/shard_map/ppermute | solution.py:48
  31.3 0.5 collective-permute-start.2
  31.8 7.5 %collective-permute-done.refs_1_ = bf16[128,1024]{1,0:T(8,128)(2,1)S(1)} collective-permute-done((bf16[128,1024]{1,0:T(8,128)(2,1)S(1)}, bf16[128,1024]{1,0:T(8,128)(2,1)S(1)}, u32[]{:S(2)}, u32[]{:S(2)}) %collective-permute-start) | collective-permute-done | bytes 262176 | tf_op jit(solution)/shard_map/ppermute | solution.py:48
  39.3 9.9 %collective-permute-done.1.refs_2_ = bf16[128,1024]{1,0:T(8,128)(2,1)S(1)} collective-permute-done((bf16[128,1024]{1,0:T(8,128)(2,1)S(1)}, bf16[128,1024]{1,0:T(8,128)(2,1)S(1)}, u32[]{:S(2)}, u32[]{:S(2)}) %collective-permute-start.1) | collective-permute-done | bytes 262176 | tf_op jit(solution)/shard_map/ppermute | solution.py:48
  49.2 4.5 %collective-permute-done.2.refs_3_ = bf16[128,1024]{1,0:T(8,128)(2,1)S(1)} collective-permute-done((bf16[128,1024]{1,0:T(8,128)(2,1)S(1)}, bf16[128,1024]{1,0:T(8,128)(2,1)S(1)}, u32[]{:S(2)}, u32[]{:S(2)}) %collective-permute-start.2) | collective-permute-done | bytes 262176 | tf_op jit(solution)/shard_map/ppermute | solution.py:48
  53.7 0.0 collective-permute-done.6.refs_5_
  53.7 2.1 %project.1 = (bf16[384,1024]{1,0:T(8,128)(2,1)}, bf16[512,384]{1,0:T(8,128)(2,1)}) custom-call(s32[4]{0:T(128)S(1)} %pad_add_fusion.place_ref, bf16[128,1024]{1,0:T(8,128)(2,1)S(1)} %get-tuple-element.8.refs_0_, bf16[128,1024]{1,0:T(8,128)(2,1)S(1)} %collective-permute-done.refs_1_, bf16[128,1024]{1,0:T(8,128)(2,1)S(1)} %collective-permute-done.1.refs_2_, ...), custom_call_target="tpu_custom_call" | custom-call | flops 402653184 | bytes 3801088 | tf_op jit(solution)/shard_map/project/pallas_call | solution.py:174
  (1 shorter events, 0.0 us)
Async XLA Ops:
  0.7 19.8 %copy-start = (bf16[1,1,384,1024]{3,2,1,0:T(8,128)(2,1)S(1)}, bf16[1,1,384,1024]{3,2,1,0:T(8,128)(2,1)}, u32[]{:S(2)}) copy-start(bf16[1,1,384,1024]{3,2,1,0:T(8,128)(2,1)} %param.5) | copy-start | bytes 2359300
  2.0 12.7 %collective-permute-start.5 = (bf16[96,1024]{1,0:T(8,128)(2,1)S(1)}, bf16[96,1024]{1,0:T(8,128)(2,1)S(1)}, u32[]{:S(2)}, u32[]{:S(2)}) collective-permute-start(bf16[96,1024]{1,0:T(8,128)(2,1)S(1)} %get-tuple-element.14), channel_id=1, source_target_pairs={{0,3},{1,2},{2,1},{3,0},{4,7},{5,6},{6,5},{7,4},{8,11},{9,10},{10,... | collective-permute-start | bytes 589832 | tf_op jit(solution)/shard_map/ppermute | solution.py:48
  3.6 12.4 %collective-permute-start.3 = (bf16[96,1024]{1,0:T(8,128)(2,1)S(1)}, bf16[96,1024]{1,0:T(8,128)(2,1)S(1)}, u32[]{:S(2)}, u32[]{:S(2)}) collective-permute-start(bf16[96,1024]{1,0:T(8,128)(2,1)S(1)} %get-tuple-element.15), channel_id=1, source_target_pairs={{0,1},{1,0},{2,3},{3,2},{4,5},{5,4},{6,7},{7,6},{8,9},{9,8},{10,11... | collective-permute-start | bytes 589832 | tf_op jit(solution)/shard_map/ppermute | solution.py:48
  6.1 14.3 %collective-permute-start.4 = (bf16[96,1024]{1,0:T(8,128)(2,1)S(1)}, bf16[96,1024]{1,0:T(8,128)(2,1)S(1)}, u32[]{:S(2)}, u32[]{:S(2)}) collective-permute-start(bf16[96,1024]{1,0:T(8,128)(2,1)S(1)} %get-tuple-element.17), channel_id=1, source_target_pairs={{0,2},{1,3},{2,0},{3,1},{4,6},{5,7},{6,4},{7,5},{8,10},{9,11},{10,... | collective-permute-start | bytes 589832 | tf_op jit(solution)/shard_map/ppermute | solution.py:48
  20.5 5.1 %copy-start.1 = (bf16[1,256,1024]{2,1,0:T(8,128)(2,1)S(1)}, bf16[1,256,1024]{2,1,0:T(8,128)(2,1)}, u32[]{:S(2)}) copy-start(bf16[1,256,1024]{2,1,0:T(8,128)(2,1)} %param.6) | copy-start | bytes 1572868
  23.9 29.8 %collective-permute-start.6 = (bf16[384,1024]{1,0:T(8,128)(2,1)S(1)}, bf16[384,1024]{1,0:T(8,128)(2,1)S(1)}, u32[]{:S(2)}, u32[]{:S(2)}) collective-permute-start(bf16[384,1024]{1,0:T(8,128)(2,1)S(1)} %update.1.refs_4_), channel_id=1, source_target_pairs={{0,16},{4,20},{8,24},{12,28},{16,0},{20,4},{24,8},{28,12},{1,17},{... | collective-permute-start | bytes 2359304 | tf_op jit(solution)/shard_map/ppermute | solution.py:171
  25.5 0.7 %copy-start.2 = (s32[1,256,1]{1,2,0:T(1,128)S(1)}, s32[1,256,1]{1,2,0:T(1,128)}, u32[]{:S(2)}) copy-start(s32[1,256,1]{1,2,0:T(1,128)} %param.7) | copy-start | bytes 3076
  27.8 11.5 %collective-permute-start = (bf16[128,1024]{1,0:T(8,128)(2,1)S(1)}, bf16[128,1024]{1,0:T(8,128)(2,1)S(1)}, u32[]{:S(2)}, u32[]{:S(2)}) collective-permute-start(bf16[128,1024]{1,0:T(8,128)(2,1)S(1)} %get-tuple-element.9), channel_id=1, source_target_pairs={{0,1},{1,0},{2,3},{3,2},{4,5},{5,4},{6,7},{7,6},{8,9},{9,8},{10,11... | collective-permute-start | bytes 786440 | tf_op jit(solution)/shard_map/ppermute | solution.py:48
  30.2 19.0 %collective-permute-start.1 = (bf16[128,1024]{1,0:T(8,128)(2,1)S(1)}, bf16[128,1024]{1,0:T(8,128)(2,1)S(1)}, u32[]{:S(2)}, u32[]{:S(2)}) collective-permute-start(bf16[128,1024]{1,0:T(8,128)(2,1)S(1)} %get-tuple-element.10), channel_id=1, source_target_pairs={{0,2},{1,3},{2,0},{3,1},{4,6},{5,7},{6,4},{7,5},{8,10},{9,11},{10,... | collective-permute-start | bytes 786440 | tf_op jit(solution)/shard_map/ppermute | solution.py:48
  31.3 22.4 %collective-permute-start.2 = (bf16[128,1024]{1,0:T(8,128)(2,1)S(1)}, bf16[128,1024]{1,0:T(8,128)(2,1)S(1)}, u32[]{:S(2)}, u32[]{:S(2)}) collective-permute-start(bf16[128,1024]{1,0:T(8,128)(2,1)S(1)} %get-tuple-element.11), channel_id=1, source_target_pairs={{0,3},{1,2},{2,1},{3,0},{4,7},{5,6},{6,5},{7,4},{8,11},{9,10},{10,... | collective-permute-start | bytes 786440 | tf_op jit(solution)/shard_map/ppermute | solution.py:48
where the time goes:
time: 55.9 us; the launch traced here: 55.8 us
  waiting for transfers between devices  36.2 us (65%)
  starting transfers between devices  9.73 us (17%)
  Pallas kernels  7.09 us (13%)
  local copies, waits for them, and re-layouts  2.02 us (4%)
  between operations  0.69 us (1%)
    ppermute x6, waiting for transfers between devices, trade(): return lax.ppermute(block, 'fsdp', pairs)  36.2 us
    ppermute x6, starting transfers between devices, trade(): return lax.ppermute(block, 'fsdp', pairs)  8.12 us
    pallas_call x1, Pallas kernels, per_device(): pl.pallas_call(functools.partial(update_kernel, nodes, width), out_shape=...  3.47 us
    pallas_call x1, Pallas kernels, per_device(): pl.pallas_call(functools.partial(project_kernel, nodes, width), out_shape...  2.08 us
    ppermute x1, starting transfers between devices, per_device(): lax.ppermute(updated, 'replica', [(i, i ^ 1 << GOSSIP_BIT) for i in range...  1.6 us
    pallas_call x1, Pallas kernels, per_device(): pl.pallas_call(functools.partial(pack_kernel, nodes, capacity), out_shape...  1.53 us
    squeeze x1, local copies, waits for them, and re-layouts, per_device(): lax.dynamic_index_in_dim(momentum[0], place[k], 0, False)  1.34 us
  transfers between devices with their start and end apart: 7, of which 6 were waited for; matrix products, arithmetic and copies ran while one was open for 0% of the time, Pallas kernels for 3%

commit v1 on v0

v1 whole, which is shorter than its diff:
```python
import functools
import math

import jax
import jax.numpy as jnp
from jax import lax
from jax.experimental import pallas as pl
from jax.experimental.pallas import tpu as pltpu
from jax.sharding import PartitionSpec as P


ITERS = 2
GOSSIP_BIT = 2


coef_a = 3.4445
coef_b = -4.775
coef_c = 2.0315
step_rate = 0.5
MH = (2, 3, 1)
TH = (1, 2, 3)
STEPS = {
    1: (1, 0, 3, 2),
    2: (2, 3, 0, 1),
    3: (3, 2, 1, 0),
    "a1": (1, 2, 3, 0),
    "a3": (3, 0, 1, 2),
    "b1": (1, 3, 0, 2),
    "b3": (2, 0, 3, 1),
    "c1": (2, 3, 1, 0),
    "c3": (3, 2, 0, 1),
}

VMEM = pl.BlockSpec(memory_space=pltpu.VMEM)


def dot(a, b):
    return jnp.dot(a, b, preferred_element_type=jnp.float32)


def dot_t(a, b):
    return lax.dot_general(a, b, (((1,), (1,)), ((), ())), preferred_element_type=jnp.float32)


def steps(nodes, order):
    if nodes == 4:
        return [STEPS[k] for k in order]
    if nodes & (nodes - 1) == 0:
        return [tuple(i ^ k for i in range(nodes)) for k in (*range(2, nodes), 1)]
    return [tuple((i + k) % nodes for i in range(nodes)) for k in (*range(2, nodes), 1)]


def inverse(step):
    return tuple(step.index(i) for i in range(len(step)))


def at(step, me):
    hop = step[0]
    if all(to == i ^ hop for i, to in enumerate(step)):
        return me ^ hop
    found = step[0]
    for i, to in enumerate(step[1:], 1):
        found = jnp.where(me == i, to, found)
    return found


def trade(block, step):
    return lax.ppermute(block, "fsdp", list(enumerate(step)))


def slice_kernel(step, source_ref, out_ref, sem):
    cp = pltpu.make_async_copy(source_ref.at[at(step, lax.axis_index("fsdp"))], out_ref, sem)
    cp.start()
    cp.wait()


def pack_kernel(to, capacity, routes_ref, tokens_ref, *out_refs):
    tok_rows = routes_ref.shape[1]
    routes = routes_ref[...]
    me = lax.axis_index("fsdp")
    earlier = lax.broadcasted_iota(jnp.int32, (tok_rows, tok_rows), 0) < lax.broadcasted_iota(
        jnp.int32, (tok_rows, tok_rows), 1
    )
    earlier = jnp.where(earlier, 1.0, 0.0).astype(jnp.bfloat16)
    slot = lax.broadcasted_iota(jnp.int32, (capacity, tok_rows), 0)
    tokens = tokens_ref[...]
    for k, step in enumerate(to):
        here = routes == at(step, me)
        count = dot(jnp.where(here, 1.0, 0.0).astype(jnp.bfloat16), earlier)
        position = jnp.where(here, count.astype(jnp.int32), -1)
        placing = jnp.where(slot == position, 1.0, 0.0).astype(jnp.bfloat16)
        out_refs[k][...] = dot(placing, tokens).astype(jnp.bfloat16)


def row_parts(rows):
    part = 128 if rows % 128 == 0 else rows
    return [slice(i, i + part) for i in range(0, rows, part)]


def update_kernel(come, width, *refs):
    nodes = len(come)
    blocks, weight_ref, out_ref, x_ref = refs[:nodes], refs[nodes], refs[nodes + 1], refs[nodes + 2]
    me = lax.axis_index("fsdp")
    rows = blocks[0].shape[0]
    total = nodes * rows
    for k in range(nodes):
        x_ref[k * rows : (k + 1) * rows, :] = blocks[k][...]
    x = x_ref[...]
    gram = dot_t(x, x)
    on_diagonal = lax.broadcasted_iota(jnp.int32, (total, total), 0) == lax.broadcasted_iota(
        jnp.int32, (total, total), 1
    )
    square = jnp.sum(jnp.where(on_diagonal, gram, 0.0))
    scale = 1.0 / (jnp.sqrt(jnp.full((1, 1), square, jnp.float32)) + 1e-07)
    gram = gram * scale * scale
    parts = row_parts(total)
    now = [gram[r] for r in parts]
    ortho = x
    for step in range(ITERS):
        low = [g.astype(jnp.bfloat16) for g in now]
        whole = jnp.concatenate(low, 0)
        poly = [coef_b * g + coef_c * dot(h, whole) for g, h in zip(now, low)]
        poly_low = [p.astype(jnp.bfloat16) for p in poly]
        poly_whole = jnp.concatenate(poly_low, 0)
        if step + 1 < ITERS:
            half = [coef_a * g + dot(p, whole) for g, p in zip(now, poly_low)]
            now = [coef_a * h + dot(h.astype(jnp.bfloat16), poly_whole) for h in half]
            ortho = (coef_a * ortho.astype(jnp.float32) + dot(poly_whole, ortho)).astype(jnp.bfloat16)
    rate = step_rate * math.sqrt(width)
    for k in range(nodes):
        r = slice(k * rows, (k + 1) * rows)
        change = dot(poly_whole[r], ortho) + coef_a * ortho[r].astype(jnp.float32)
        home = pl.ds(pl.multiple_of(at(come[k], me) * rows, rows), rows)
        out_ref[home, :] = (
            weight_ref[home, :].astype(jnp.float32) - (rate * scale) * change
        ).astype(jnp.bfloat16)


def project_kernel(come, width, *refs):
    nodes = len(come)
    me = lax.axis_index("fsdp")
    blocks, own_ref, partner_ref = refs[:nodes], refs[nodes], refs[nodes + 1]
    weight_ref, rows_ref, slot_ref = refs[nodes + 2], refs[nodes + 3], refs[nodes + 4]
    capacity = blocks[0].shape[0]
    weight = (
        0.5 * (own_ref[...].astype(jnp.float32) + partner_ref[...].astype(jnp.float32))
    ).astype(jnp.bfloat16)
    weight_ref[...] = weight
    for k in range(nodes):
        home = pl.ds(pl.multiple_of(at(come[k], me) * capacity, capacity), capacity)
        slot_ref[home, :] = blocks[k][...]
    rows_ref[...] = (dot_t(slot_ref[...], weight) * (1.0 / math.sqrt(width))).astype(jnp.bfloat16)


def per_device(momentum, weights, tokens, routes):
    nodes = lax.axis_size("fsdp")
    rows, width = momentum.shape[2], momentum.shape[3]
    total = weights.shape[2]
    tok_rows = tokens.shape[1]
    capacity = 2 * tok_rows // nodes
    here = tuple(range(nodes))
    far = [here, *steps(nodes, MH)]
    near = [here, *steps(nodes, TH)]

    source = pltpu.with_memory_space_constraint(momentum[0], pltpu.HBM)
    blocks = []
    for k, step in enumerate(far):
        shard = pl.pallas_call(
            functools.partial(slice_kernel, step),
            out_shape=jax.ShapeDtypeStruct((rows, width), jnp.bfloat16),
            in_specs=[pl.BlockSpec(memory_space=pltpu.HBM)],
            out_specs=VMEM,
            scratch_shapes=[pltpu.SemaphoreType.DMA],
            compiler_params=pltpu.CompilerParams(vmem_limit_bytes=8 << 20),
            name="slice",
        )(source)
        blocks.append(trade(shard, step) if k else shard)

    packed = list(
        pl.pallas_call(
            functools.partial(pack_kernel, near, capacity),
            out_shape=[jax.ShapeDtypeStruct((capacity, width), jnp.bfloat16)] * nodes,
            in_specs=[VMEM, VMEM],
            out_specs=[VMEM] * nodes,
            compiler_params=pltpu.CompilerParams(vmem_limit_bytes=16 << 20),
            cost_estimate=pl.CostEstimate(
                flops=2 * nodes * capacity * tok_rows * width,
                bytes_accessed=2 * (tok_rows + nodes * capacity) * width,
                transcendentals=0,
            ),
            name="pack",
        )(routes.reshape(1, tok_rows), tokens[0])
    )
    slots = [packed[0]]
    for k, step in enumerate(near[1:], 1):
        slots.append(trade(packed[k], step))

    updated = pl.pallas_call(
        functools.partial(update_kernel, [inverse(s) for s in far], width),
        out_shape=jax.ShapeDtypeStruct((total, width), jnp.bfloat16),
        in_specs=[VMEM] * (nodes + 1),
        out_specs=VMEM,
        scratch_shapes=[pltpu.VMEM((total, width), jnp.bfloat16)],
        compiler_params=pltpu.CompilerParams(vmem_limit_bytes=24 << 20),
        cost_estimate=pl.CostEstimate(
            flops=4 * total * total * width + 10 * total**3,
            bytes_accessed=6 * total * width,
            transcendentals=0,
        ),
        name="update",
    )(*blocks, weights[0, 0])
    partner = lax.ppermute(
        updated, "replica", [(i, i ^ 1 << GOSSIP_BIT) for i in range(lax.axis_size("replica"))]
    )
    averaged, expert_rows = pl.pallas_call(
        functools.partial(project_kernel, [inverse(s) for s in near], width),
        out_shape=(
            jax.ShapeDtypeStruct((total, width), jnp.bfloat16),
            jax.ShapeDtypeStruct((nodes * capacity, total), jnp.bfloat16),
        ),
        in_specs=[VMEM] * (nodes + 2),
        out_specs=(VMEM, VMEM),
        scratch_shapes=[pltpu.VMEM((nodes * capacity, width), jnp.bfloat16)],
        compiler_params=pltpu.CompilerParams(vmem_limit_bytes=24 << 20),
        cost_estimate=pl.CostEstimate(
            flops=2 * nodes * capacity * width * total,
            bytes_accessed=6 * total * width + 2 * nodes * capacity * (width + total),
            transcendentals=0,
        ),
        name="project",
    )(*slots, updated, partner)
    return (averaged[None, None], expert_rows[None, None])


def solution(mesh):
    in_specs = (
        P("replica", None, "fsdp", None),
        P("replica", "fsdp", None, None),
        P("replica", "fsdp", None),
        P("replica", "fsdp", None),
    )
    out_specs = (P("replica", "fsdp", None, None), P("replica", "fsdp", None, None))

    return jax.shard_map(per_device, mesh=mesh, in_specs=in_specs, out_specs=out_specs, check_vma=False)
```

time: 55.9 us -> 55.7 us (level)
  the two profiles are of different devices: /device:TPU:8 before, /device:TPU:16 now
where the time goes in v1:
time: 55.7 us; the launch traced here: 55.4 us
  waiting for transfers between devices  35.4 us (64%)
  starting transfers between devices  9.7 us (17%)
  Pallas kernels  8.92 us (16%)
  between operations  0.7 us (1%)
  local copies, waits for them, and re-layouts  0.69 us (1%)
    ppermute x6, waiting for transfers between devices, trade(): return lax.ppermute(block, 'fsdp', list(enumerate(step)))  35.4 us
    ppermute x6, starting transfers between devices, trade(): return lax.ppermute(block, 'fsdp', list(enumerate(step)))  8.12 us
    pallas_call x4, Pallas kernels, per_device(): pl.pallas_call(functools.partial(slice_kernel, step), out_shape=jax.Shape...  3.76 us
    pallas_call x1, Pallas kernels, per_device(): pl.pallas_call(functools.partial(update_kernel, [inverse(s) for s in far]...  2.62 us
    ppermute x1, starting transfers between devices, per_device(): lax.ppermute(updated, 'replica', [(i, i ^ 1 << GOSSIP_BIT) for i in range...  1.58 us
    pallas_call x1, Pallas kernels, per_device(): pl.pallas_call(functools.partial(project_kernel, [inverse(s) for s in nea...  1.54 us
  transfers between devices with their start and end apart: 7, of which 5 were waited for; matrix products, arithmetic and copies ran while one was open for 0% of the time, Pallas kernels for 7%

profile of v1, /device:TPU:16, one launch (start us, length us, event | category | flops | bytes accessed | tf_op | source)
XLA Modules:
  0.0 55.4 jit_solution(10920573383516795625)
XLA Ops:
  0.6 0.9 %slice.5 = bf16[96,1024]{1,0:T(8,128)(2,1)S(1)} custom-call(bf16[4,96,1024]{2,1,0:T(8,128)(2,1)} %bitcast.9), custom_call_target="tpu_custom_call" | custom-call | tf_op jit(solution)/shard_map/slice/pallas_call | solution.py:168
  1.6 0.1 collective-permute-start.3
  1.7 0.9 %slice.6 = bf16[96,1024]{1,0:T(8,128)(2,1)S(1)} custom-call(bf16[4,96,1024]{2,1,0:T(8,128)(2,1)} %bitcast.10), custom_call_target="tpu_custom_call" | custom-call | tf_op jit(solution)/shard_map/slice/pallas_call | solution.py:168
  2.6 0.0 copy-start
  2.6 3.1 %collective-permute-start.4 = (bf16[96,1024]{1,0:T(8,128)(2,1)S(1)}, bf16[96,1024]{1,0:T(8,128)(2,1)S(1)}, u32[]{:S(2)}, u32[]{:S(2)}) collective-permute-start(bf16[96,1024]{1,0:T(8,128)(2,1)S(1)} %slice.6), channel_id=1, source_target_pairs={{0,3},{1,2},{2,1},{3,0},{4,7},{5,6},{6,5},{7,4},{8,11},{9,10},{10,... | collective-permute-start | bytes 589832 | tf_op jit(solution)/shard_map/ppermute | solution.py:68
  5.7 0.9 %slice.7 = bf16[96,1024]{1,0:T(8,128)(2,1)S(1)} custom-call(bf16[4,96,1024]{2,1,0:T(8,128)(2,1)} %bitcast.11), custom_call_target="tpu_custom_call" | custom-call | tf_op jit(solution)/shard_map/slice/pallas_call | solution.py:168
  6.6 1.4 %collective-permute-start.5 = (bf16[96,1024]{1,0:T(8,128)(2,1)S(1)}, bf16[96,1024]{1,0:T(8,128)(2,1)S(1)}, u32[]{:S(2)}, u32[]{:S(2)}) collective-permute-start(bf16[96,1024]{1,0:T(8,128)(2,1)S(1)} %slice.7), channel_id=1, source_target_pairs={{0,1},{1,0},{2,3},{3,2},{4,5},{5,4},{6,7},{7,6},{8,9},{9,8},{10,11... | collective-permute-start | bytes 589832 | tf_op jit(solution)/shard_map/ppermute | solution.py:68
  8.1 0.9 %slice.4.refs_0_ = bf16[96,1024]{1,0:T(8,128)(2,1)S(1)} custom-call(bf16[4,96,1024]{2,1,0:T(8,128)(2,1)} %bitcast.12), custom_call_target="tpu_custom_call" | custom-call | tf_op jit(solution)/shard_map/slice/pallas_call | solution.py:168
  9.0 6.4 %collective-permute-done.3.refs_1_ = bf16[96,1024]{1,0:T(8,128)(2,1)S(1)} collective-permute-done((bf16[96,1024]{1,0:T(8,128)(2,1)S(1)}, bf16[96,1024]{1,0:T(8,128)(2,1)S(1)}, u32[]{:S(2)}, u32[]{:S(2)}) %collective-permute-start.3) | collective-permute-done | bytes 196640 | tf_op jit(solution)/shard_map/ppermute | solution.py:68
  15.4 6.5 %collective-permute-done.4.refs_2_ = bf16[96,1024]{1,0:T(8,128)(2,1)S(1)} collective-permute-done((bf16[96,1024]{1,0:T(8,128)(2,1)S(1)}, bf16[96,1024]{1,0:T(8,128)(2,1)S(1)}, u32[]{:S(2)}, u32[]{:S(2)}) %collective-permute-start.4) | collective-permute-done | bytes 196640 | tf_op jit(solution)/shard_map/ppermute | solution.py:68
  21.9 0.0 collective-permute-done.5.refs_3_
  21.9 0.0 copy-done
  21.9 2.6 %update.1.refs_4_ = bf16[384,1024]{1,0:T(8,128)(2,1)S(1)} custom-call(bf16[96,1024]{1,0:T(8,128)(2,1)S(1)} %slice.4.refs_0_, bf16[96,1024]{1,0:T(8,128)(2,1)S(1)} %collective-permute-done.3.refs_1_, bf16[96,1024]{1,0:T(8,128)(2,1)S(1)} %collective-permute-done.4.refs_2_, bf16[96,1024]{1,0:T(8,128)(2,1)S(1)} %collective-permute-done.5.refs_3_, ...), custom_call_target="tpu_custom_call" | custom-call | flops 1170210816 | bytes 2359296 | tf_op jit(solution)/shard_map/update/pallas_call | solution.py:198
  24.5 1.6 %collective-permute-start.6 = (bf16[384,1024]{1,0:T(8,128)(2,1)S(1)}, bf16[384,1024]{1,0:T(8,128)(2,1)S(1)}, u32[]{:S(2)}, u32[]{:S(2)}) collective-permute-start(bf16[384,1024]{1,0:T(8,128)(2,1)S(1)} %update.1.refs_4_), channel_id=1, source_target_pairs={{0,16},{4,20},{8,24},{12,28},{16,0},{20,4},{24,8},{28,12},{1,17},{... | collective-permute-start | bytes 2359304 | tf_op jit(solution)/shard_map/ppermute | solution.py:212
  26.1 0.7 %copy-done.2 = s32[1,256,1]{1,2,0:T(1,128)S(1)} copy-done((s32[1,256,1]{1,2,0:T(1,128)S(1)}, s32[1,256,1]{1,2,0:T(1,128)}, u32[]{:S(2)}) %copy-start.2) | copy-done | bytes 1048
  26.8 1.0 %pack.1 = (bf16[128,1024]{1,0:T(8,128)(2,1)S(1)}, bf16[128,1024]{1,0:T(8,128)(2,1)S(1)}, bf16[128,1024]{1,0:T(8,128)(2,1)S(1)}, bf16[128,1024]{1,0:T(8,128)(2,1)S(1)}) custom-call(s32[1,256]{1,0:T(1,128)S(1)} %bitcast.8, bf16[256,1024]{1,0:T(8,128)(2,1)S(1)} %bitcast.7), custom_call_target="tpu_custom_call" | custom-call | flops 268435456 | bytes 1572864 | tf_op jit(solution)/shard_map/pack/pallas_call | solution.py:180
  27.8 0.5 collective-permute-start
  28.3 0.6 %collective-permute-start.1 = (bf16[128,1024]{1,0:T(8,128)(2,1)S(1)}, bf16[128,1024]{1,0:T(8,128)(2,1)S(1)}, u32[]{:S(2)}, u32[]{:S(2)}) collective-permute-start(bf16[128,1024]{1,0:T(8,128)(2,1)S(1)} %get-tuple-element.10), channel_id=1, source_target_pairs={{0,2},{1,3},{2,0},{3,1},{4,6},{5,7},{6,4},{7,5},{8,10},{9,11},{10,... | collective-permute-start | bytes 786440 | tf_op jit(solution)/shard_map/ppermute | solution.py:68
  28.8 2.5 %collective-permute-start.2 = (bf16[128,1024]{1,0:T(8,128)(2,1)S(1)}, bf16[128,1024]{1,0:T(8,128)(2,1)S(1)}, u32[]{:S(2)}, u32[]{:S(2)}) collective-permute-start(bf16[128,1024]{1,0:T(8,128)(2,1)S(1)} %get-tuple-element.11), channel_id=1, source_target_pairs={{0,3},{1,2},{2,1},{3,0},{4,7},{5,6},{6,5},{7,4},{8,11},{9,10},{10,... | collective-permute-start | bytes 786440 | tf_op jit(solution)/shard_map/ppermute | solution.py:68
  31.3 5.7 %collective-permute-done.refs_1_ = bf16[128,1024]{1,0:T(8,128)(2,1)S(1)} collective-permute-done((bf16[128,1024]{1,0:T(8,128)(2,1)S(1)}, bf16[128,1024]{1,0:T(8,128)(2,1)S(1)}, u32[]{:S(2)}, u32[]{:S(2)}) %collective-permute-start) | collective-permute-done | bytes 262176 | tf_op jit(solution)/shard_map/ppermute | solution.py:68
  37.1 9.6 %collective-permute-done.1.refs_2_ = bf16[128,1024]{1,0:T(8,128)(2,1)S(1)} collective-permute-done((bf16[128,1024]{1,0:T(8,128)(2,1)S(1)}, bf16[128,1024]{1,0:T(8,128)(2,1)S(1)}, u32[]{:S(2)}, u32[]{:S(2)}) %collective-permute-start.1) | collective-permute-done | bytes 262176 | tf_op jit(solution)/shard_map/ppermute | solution.py:68
  46.6 7.2 %collective-permute-done.2.refs_3_ = bf16[128,1024]{1,0:T(8,128)(2,1)S(1)} collective-permute-done((bf16[128,1024]{1,0:T(8,128)(2,1)S(1)}, bf16[128,1024]{1,0:T(8,128)(2,1)S(1)}, u32[]{:S(2)}, u32[]{:S(2)}) %collective-permute-start.2) | collective-permute-done | bytes 262176 | tf_op jit(solution)/shard_map/ppermute | solution.py:68
  53.9 0.0 collective-permute-done.6.refs_5_
  53.9 1.5 %project.1 = (bf16[384,1024]{1,0:T(8,128)(2,1)}, bf16[512,384]{1,0:T(8,128)(2,1)}) custom-call(bf16[128,1024]{1,0:T(8,128)(2,1)S(1)} %get-tuple-element.8.refs_0_, bf16[128,1024]{1,0:T(8,128)(2,1)S(1)} %collective-permute-done.refs_1_, bf16[128,1024]{1,0:T(8,128)(2,1)S(1)} %collective-permute-done.1.refs_2_, ...), custom_call_target="tpu_custom_call" | custom-call | flops 402653184 | bytes 3801088 | tf_op jit(solution)/shard_map/project/pallas_call | solution.py:215
  (3 shorter events, 0.0 us)
Async XLA Ops:
  1.6 13.8 %collective-permute-start.3 = (bf16[96,1024]{1,0:T(8,128)(2,1)S(1)}, bf16[96,1024]{1,0:T(8,128)(2,1)S(1)}, u32[]{:S(2)}, u32[]{:S(2)}) collective-permute-start(bf16[96,1024]{1,0:T(8,128)(2,1)S(1)} %slice.5), channel_id=1, source_target_pairs={{0,2},{1,3},{2,0},{3,1},{4,6},{5,7},{6,4},{7,5},{8,10},{9,11},{10,... | collective-permute-start | bytes 589832 | tf_op jit(solution)/shard_map/ppermute | solution.py:68
  2.6 19.3 %copy-start = (bf16[1,1,384,1024]{3,2,1,0:T(8,128)(2,1)S(1)}, bf16[1,1,384,1024]{3,2,1,0:T(8,128)(2,1)}, u32[]{:S(2)}) copy-start(bf16[1,1,384,1024]{3,2,1,0:T(8,128)(2,1)} %param.5) | copy-start | bytes 2359300
  2.6 19.2 %collective-permute-start.4 = (bf16[96,1024]{1,0:T(8,128)(2,1)S(1)}, bf16[96,1024]{1,0:T(8,128)(2,1)S(1)}, u32[]{:S(2)}, u32[]{:S(2)}) collective-permute-start(bf16[96,1024]{1,0:T(8,128)(2,1)S(1)} %slice.6), channel_id=1, source_target_pairs={{0,3},{1,2},{2,1},{3,0},{4,7},{5,6},{6,5},{7,4},{8,11},{9,10},{10,... | collective-permute-start | bytes 589832 | tf_op jit(solution)/shard_map/ppermute | solution.py:68
  6.6 15.2 %collective-permute-start.5 = (bf16[96,1024]{1,0:T(8,128)(2,1)S(1)}, bf16[96,1024]{1,0:T(8,128)(2,1)S(1)}, u32[]{:S(2)}, u32[]{:S(2)}) collective-permute-start(bf16[96,1024]{1,0:T(8,128)(2,1)S(1)} %slice.7), channel_id=1, source_target_pairs={{0,1},{1,0},{2,3},{3,2},{4,5},{5,4},{6,7},{7,6},{8,9},{9,8},{10,11... | collective-permute-start | bytes 589832 | tf_op jit(solution)/shard_map/ppermute | solution.py:68
  21.9 4.2 %copy-start.1 = (bf16[1,256,1024]{2,1,0:T(8,128)(2,1)S(1)}, bf16[1,256,1024]{2,1,0:T(8,128)(2,1)}, u32[]{:S(2)}) copy-start(bf16[1,256,1024]{2,1,0:T(8,128)(2,1)} %param.6) | copy-start | bytes 1572868
  24.5 29.4 %collective-permute-start.6 = (bf16[384,1024]{1,0:T(8,128)(2,1)S(1)}, bf16[384,1024]{1,0:T(8,128)(2,1)S(1)}, u32[]{:S(2)}, u32[]{:S(2)}) collective-permute-start(bf16[384,1024]{1,0:T(8,128)(2,1)S(1)} %update.1.refs_4_), channel_id=1, source_target_pairs={{0,16},{4,20},{8,24},{12,28},{16,0},{20,4},{24,8},{28,12},{1,17},{... | collective-permute-start | bytes 2359304 | tf_op jit(solution)/shard_map/ppermute | solution.py:212
  26.1 0.7 %copy-start.2 = (s32[1,256,1]{1,2,0:T(1,128)S(1)}, s32[1,256,1]{1,2,0:T(1,128)}, u32[]{:S(2)}) copy-start(s32[1,256,1]{1,2,0:T(1,128)} %param.7) | copy-start | bytes 3076
  27.8 9.3 %collective-permute-start = (bf16[128,1024]{1,0:T(8,128)(2,1)S(1)}, bf16[128,1024]{1,0:T(8,128)(2,1)S(1)}, u32[]{:S(2)}, u32[]{:S(2)}) collective-permute-start(bf16[128,1024]{1,0:T(8,128)(2,1)S(1)} %get-tuple-element.9), channel_id=1, source_target_pairs={{0,1},{1,0},{2,3},{3,2},{4,5},{5,4},{6,7},{7,6},{8,9},{9,8},{10,11... | collective-permute-start | bytes 786440 | tf_op jit(solution)/shard_map/ppermute | solution.py:68
  28.3 18.4 %collective-permute-start.1 = (bf16[128,1024]{1,0:T(8,128)(2,1)S(1)}, bf16[128,1024]{1,0:T(8,128)(2,1)S(1)}, u32[]{:S(2)}, u32[]{:S(2)}) collective-permute-start(bf16[128,1024]{1,0:T(8,128)(2,1)S(1)} %get-tuple-element.10), channel_id=1, source_target_pairs={{0,2},{1,3},{2,0},{3,1},{4,6},{5,7},{6,4},{7,5},{8,10},{9,11},{10,... | collective-permute-start | bytes 786440 | tf_op jit(solution)/shard_map/ppermute | solution.py:68
  28.8 25.0 %collective-permute-start.2 = (bf16[128,1024]{1,0:T(8,128)(2,1)S(1)}, bf16[128,1024]{1,0:T(8,128)(2,1)S(1)}, u32[]{:S(2)}, u32[]{:S(2)}) collective-permute-start(bf16[128,1024]{1,0:T(8,128)(2,1)S(1)} %get-tuple-element.11), channel_id=1, source_target_pairs={{0,3},{1,2},{2,1},{3,0},{4,7},{5,6},{6,5},{7,4},{8,11},{9,10},{10,... | collective-permute-start | bytes 786440 | tf_op jit(solution)/shard_map/ppermute | solution.py:68

commit v2 on v1

--- a/solution.py
+++ b/solution.py
@@ -17,7 +17,7 @@
 coef_b = -4.775
 coef_c = 2.0315
 step_rate = 0.5
-MH = (2, 3, 1)
+MH = ("c3", 1, "c1")
 TH = (1, 2, 3)
 STEPS = {
     1: (1, 0, 3, 2),
@@ -138,18 +138,41 @@
 
 def project_kernel(come, width, *refs):
     nodes = len(come)
-    me = lax.axis_index("fsdp")
     blocks, own_ref, partner_ref = refs[:nodes], refs[nodes], refs[nodes + 1]
-    weight_ref, rows_ref, slot_ref = refs[nodes + 2], refs[nodes + 3], refs[nodes + 4]
+    weight_out, rows_out, weight_ref, slot_ref, rows_ref, sems = refs[nodes + 2 :]
+    me = lax.axis_index("fsdp")
     capacity = blocks[0].shape[0]
     weight = (
         0.5 * (own_ref[...].astype(jnp.float32) + partner_ref[...].astype(jnp.float32))
     ).astype(jnp.bfloat16)
     weight_ref[...] = weight
+    copies = [pltpu.make_async_copy(weight_ref, weight_out, sems.at[nodes])]
+    copies[0].start()
+    for k in range(nodes):
+        slot_ref[k * capacity : (k + 1) * capacity, :] = blocks[k][...]
+    rows_ref[...] = (dot_t(slot_ref[...], weight) * (1.0 / math.sqrt(width))).astype(jnp.bfloat16)
     for k in range(nodes):
         home = pl.ds(pl.multiple_of(at(come[k], me) * capacity, capacity), capacity)
-        slot_ref[home, :] = blocks[k][...]
-    rows_ref[...] = (dot_t(slot_ref[...], weight) * (1.0 / math.sqrt(width))).astype(jnp.bfloat16)
+        copies.append(
+            pltpu.make_async_copy(
+                rows_ref.at[k * capacity : (k + 1) * capacity], rows_out.at[home], sems.at[k]
+            )
+        )
+        copies[-1].start()
+    for cp in copies:
+        cp.wait()
+
+
+def last_kernel(come, width, block_ref, weight_ref, _, rows_out, rows_ref, sem):
+    me = lax.axis_index("fsdp")
+    capacity = block_ref.shape[0]
+    rows_ref[...] = (dot_t(block_ref[...], weight_ref[...]) * (1.0 / math.sqrt(width))).astype(
+        jnp.bfloat16
+    )
+    home = pl.ds(pl.multiple_of(at(come, me) * capacity, capacity), capacity)
+    cp = pltpu.make_async_copy(rows_ref, rows_out.at[home], sem)
+    cp.start()
+    cp.wait()
 
 
 def per_device(momentum, weights, tokens, routes):
@@ -212,23 +235,50 @@
     partner = lax.ppermute(
         updated, "replica", [(i, i ^ 1 << GOSSIP_BIT) for i in range(lax.axis_size("replica"))]
     )
-    averaged, expert_rows = pl.pallas_call(
-        functools.partial(project_kernel, [inverse(s) for s in near], width),
+    come = [inverse(step) for step in near]
+    early = nodes - 1
+    rows_shape = jax.ShapeDtypeStruct((nodes * capacity, total), jnp.bfloat16)
+    hbm = pl.BlockSpec(memory_space=pltpu.HBM)
+    averaged, expert_rows, kept = pl.pallas_call(
+        functools.partial(project_kernel, come[:early], width),
         out_shape=(
             jax.ShapeDtypeStruct((total, width), jnp.bfloat16),
-            jax.ShapeDtypeStruct((nodes * capacity, total), jnp.bfloat16),
-        ),
-        in_specs=[VMEM] * (nodes + 2),
-        out_specs=(VMEM, VMEM),
-        scratch_shapes=[pltpu.VMEM((nodes * capacity, width), jnp.bfloat16)],
+            rows_shape,
+            jax.ShapeDtypeStruct((total, width), jnp.bfloat16),
+        ),
+        in_specs=[VMEM] * (early + 2),
+        out_specs=(hbm, hbm, VMEM),
+        scratch_shapes=[
+            pltpu.VMEM((early * capacity, width), jnp.bfloat16),
+            pltpu.VMEM((early * capacity, total), jnp.bfloat16),
+            pltpu.SemaphoreType.DMA((nodes,)),
+        ],
         compiler_params=pltpu.CompilerParams(vmem_limit_bytes=24 << 20),
         cost_estimate=pl.CostEstimate(
-            flops=2 * nodes * capacity * width * total,
-            bytes_accessed=6 * total * width + 2 * nodes * capacity * (width + total),
+            flops=2 * early * capacity * width * total,
+            bytes_accessed=6 * total * width + 2 * early * capacity * (width + total),
             transcendentals=0,
         ),
         name="project",
-    )(*slots, updated, partner)
+    )(*slots[:early], updated, partner)
+    expert_rows = pl.pallas_call(
+        functools.partial(last_kernel, come[early], width),
+        out_shape=rows_shape,
+        in_specs=[VMEM, VMEM, hbm],
+        out_specs=hbm,
+        scratch_shapes=[
+            pltpu.VMEM((capacity, total), jnp.bfloat16),
+            pltpu.SemaphoreType.DMA,
+        ],
+        input_output_aliases={2: 0},
+        compiler_params=pltpu.CompilerParams(vmem_limit_bytes=24 << 20),
+        cost_estimate=pl.CostEstimate(
+            flops=2 * capacity * width * total,
+            bytes_accessed=2 * capacity * (width + total),
+            transcendentals=0,
+        ),
+        name="last",
+    )(slots[early], kept, expert_rows)
     return (averaged[None, None], expert_rows[None, None])
 
 

time: 55.7 us -> 53.8 us (0.966)
  the two profiles are of different devices: /device:TPU:16 before, /device:TPU:0 now
where the time goes in v2:
time: 53.8 us; the launch traced here: 53.6 us
  waiting for transfers between devices  29.6 us (55%)
  starting transfers between devices  12.8 us (24%)
  Pallas kernels  9.82 us (18%)
  between operations  0.72 us (1%)
  local copies, waits for them, and re-layouts  0.69 us (1%)
    ppermute x6, waiting for transfers between devices, trade(): return lax.ppermute(block, 'fsdp', list(enumerate(step)))  29.5 us
    ppermute x6, starting transfers between devices, trade(): return lax.ppermute(block, 'fsdp', list(enumerate(step)))  11.2 us
    pallas_call x4, Pallas kernels, per_device(): pl.pallas_call(functools.partial(slice_kernel, step), out_shape=jax.Shape...  3.82 us
    pallas_call x1, Pallas kernels, per_device(): pl.pallas_call(functools.partial(update_kernel, [inverse(s) for s in far]...  2.62 us
    ppermute x1, starting transfers between devices, per_device(): lax.ppermute(updated, 'replica', [(i, i ^ 1 << GOSSIP_BIT) for i in range...  1.63 us
    pallas_call x1, Pallas kernels, per_device(): pl.pallas_call(functools.partial(project_kernel, come[:early], width), ou...  1.36 us
  transfers between devices with their start and end apart: 7, of which 4 were waited for; matrix products, arithmetic and copies ran while one was open for 0% of the time, Pallas kernels for 10%

profile of v2, /device:TPU:0, one launch (start us, length us, event | category | flops | bytes accessed | tf_op | source)
XLA Modules:
  0.0 53.6 jit_solution(12347482708613679937)
XLA Ops:
  0.6 0.9 %slice.5 = bf16[96,1024]{1,0:T(8,128)(2,1)S(1)} custom-call(bf16[4,96,1024]{2,1,0:T(8,128)(2,1)} %bitcast.9), custom_call_target="tpu_custom_call" | custom-call | tf_op jit(solution)/shard_map/slice/pallas_call | solution.py:191
  1.6 5.1 %collective-permute-start.2 = (bf16[96,1024]{1,0:T(8,128)(2,1)S(1)}, bf16[96,1024]{1,0:T(8,128)(2,1)S(1)}, u32[]{:S(2)}, u32[]{:S(2)}) collective-permute-start(bf16[96,1024]{1,0:T(8,128)(2,1)S(1)} %slice.5), channel_id=1, source_target_pairs={{0,3},{1,2},{2,0},{3,1},{4,7},{5,6},{6,4},{7,5},{8,11},{9,10},{10,... | collective-permute-start | bytes 589832 | tf_op jit(solution)/shard_map/ppermute | solution.py:68
  6.7 0.9 %slice.6 = bf16[96,1024]{1,0:T(8,128)(2,1)S(1)} custom-call(bf16[4,96,1024]{2,1,0:T(8,128)(2,1)} %bitcast.10), custom_call_target="tpu_custom_call" | custom-call | tf_op jit(solution)/shard_map/slice/pallas_call | solution.py:191
  7.7 0.0 copy-start
  7.7 0.1 collective-permute-start.3
  7.7 1.0 %slice.7 = bf16[96,1024]{1,0:T(8,128)(2,1)S(1)} custom-call(bf16[4,96,1024]{2,1,0:T(8,128)(2,1)} %bitcast.11), custom_call_target="tpu_custom_call" | custom-call | tf_op jit(solution)/shard_map/slice/pallas_call | solution.py:191
  8.8 0.9 %collective-permute-start.4 = (bf16[96,1024]{1,0:T(8,128)(2,1)S(1)}, bf16[96,1024]{1,0:T(8,128)(2,1)S(1)}, u32[]{:S(2)}, u32[]{:S(2)}) collective-permute-start(bf16[96,1024]{1,0:T(8,128)(2,1)S(1)} %slice.7), channel_id=1, source_target_pairs={{0,2},{1,3},{2,1},{3,0},{4,6},{5,7},{6,5},{7,4},{8,10},{9,11},{10,... | collective-permute-start | bytes 589832 | tf_op jit(solution)/shard_map/ppermute | solution.py:68
  9.6 0.9 %slice.4.refs_0_ = bf16[96,1024]{1,0:T(8,128)(2,1)S(1)} custom-call(bf16[4,96,1024]{2,1,0:T(8,128)(2,1)} %bitcast.12), custom_call_target="tpu_custom_call" | custom-call | tf_op jit(solution)/shard_map/slice/pallas_call | solution.py:191
  10.6 6.0 %collective-permute-done.2.refs_1_ = bf16[96,1024]{1,0:T(8,128)(2,1)S(1)} collective-permute-done((bf16[96,1024]{1,0:T(8,128)(2,1)S(1)}, bf16[96,1024]{1,0:T(8,128)(2,1)S(1)}, u32[]{:S(2)}, u32[]{:S(2)}) %collective-permute-start.2) | collective-permute-done | bytes 196640 | tf_op jit(solution)/shard_map/ppermute | solution.py:68
  16.6 4.8 %collective-permute-done.3.refs_2_ = bf16[96,1024]{1,0:T(8,128)(2,1)S(1)} collective-permute-done((bf16[96,1024]{1,0:T(8,128)(2,1)S(1)}, bf16[96,1024]{1,0:T(8,128)(2,1)S(1)}, u32[]{:S(2)}, u32[]{:S(2)}) %collective-permute-start.3) | collective-permute-done | bytes 196640 | tf_op jit(solution)/shard_map/ppermute | solution.py:68
  21.4 0.0 collective-permute-done.4.refs_3_
  21.4 2.6 %update.1.refs_3_ = bf16[384,1024]{1,0:T(8,128)(2,1)S(1)} custom-call(bf16[96,1024]{1,0:T(8,128)(2,1)S(1)} %slice.4.refs_0_, bf16[96,1024]{1,0:T(8,128)(2,1)S(1)} %collective-permute-done.2.refs_1_, bf16[96,1024]{1,0:T(8,128)(2,1)S(1)} %collective-permute-done.3.refs_2_, bf16[96,1024]{1,0:T(8,128)(2,1)S(1)} %collective-permute-done.4.refs_3_, ...), custom_call_target="tpu_custom_call" | custom-call | flops 1170210816 | bytes 2359296 | tf_op jit(solution)/shard_map/update/pallas_call | solution.py:221
  24.0 1.6 %collective-permute-start.5 = (bf16[384,1024]{1,0:T(8,128)(2,1)S(1)}, bf16[384,1024]{1,0:T(8,128)(2,1)S(1)}, u32[]{:S(2)}, u32[]{:S(2)}) collective-permute-start(bf16[384,1024]{1,0:T(8,128)(2,1)S(1)} %update.1.refs_3_), channel_id=1, source_target_pairs={{0,16},{4,20},{8,24},{12,28},{16,0},{20,4},{24,8},{28,12},{1,17},{... | collective-permute-start | bytes 2359304 | tf_op jit(solution)/shard_map/ppermute | solution.py:235
  25.6 0.7 %copy-done.2 = s32[1,256,1]{1,2,0:T(1,128)S(1)} copy-done((s32[1,256,1]{1,2,0:T(1,128)S(1)}, s32[1,256,1]{1,2,0:T(1,128)}, u32[]{:S(2)}) %copy-start.2) | copy-done | bytes 1048
  26.3 1.0 %pack.1 = (bf16[128,1024]{1,0:T(8,128)(2,1)S(1)}, bf16[128,1024]{1,0:T(8,128)(2,1)S(1)}, bf16[128,1024]{1,0:T(8,128)(2,1)S(1)}, bf16[128,1024]{1,0:T(8,128)(2,1)S(1)}) custom-call(s32[1,256]{1,0:T(1,128)S(1)} %bitcast.8, bf16[256,1024]{1,0:T(8,128)(2,1)S(1)} %bitcast.7), custom_call_target="tpu_custom_call" | custom-call | flops 268435456 | bytes 1572864 | tf_op jit(solution)/shard_map/pack/pallas_call | solution.py:203
  27.3 2.5 %collective-permute-start = (bf16[128,1024]{1,0:T(8,128)(2,1)S(1)}, bf16[128,1024]{1,0:T(8,128)(2,1)S(1)}, u32[]{:S(2)}, u32[]{:S(2)}) collective-permute-start(bf16[128,1024]{1,0:T(8,128)(2,1)S(1)} %get-tuple-element.10), channel_id=1, source_target_pairs={{0,1},{1,0},{2,3},{3,2},{4,5},{5,4},{6,7},{7,6},{8,9},{9,8},{10,11... | collective-permute-start | bytes 786440 | tf_op jit(solution)/shard_map/ppermute | solution.py:68
  29.9 2.5 %collective-permute-start.1 = (bf16[128,1024]{1,0:T(8,128)(2,1)S(1)}, bf16[128,1024]{1,0:T(8,128)(2,1)S(1)}, u32[]{:S(2)}, u32[]{:S(2)}) collective-permute-start(bf16[128,1024]{1,0:T(8,128)(2,1)S(1)} %get-tuple-element.11), channel_id=1, source_target_pairs={{0,2},{1,3},{2,0},{3,1},{4,6},{5,7},{6,4},{7,5},{8,10},{9,11},{10,... | collective-permute-start | bytes 786440 | tf_op jit(solution)/shard_map/ppermute | solution.py:68
  32.4 0.0 collective-permute-start.6
  32.4 6.8 %collective-permute-done.refs_1_ = bf16[128,1024]{1,0:T(8,128)(2,1)S(1)} collective-permute-done((bf16[128,1024]{1,0:T(8,128)(2,1)S(1)}, bf16[128,1024]{1,0:T(8,128)(2,1)S(1)}, u32[]{:S(2)}, u32[]{:S(2)}) %collective-permute-start) | collective-permute-done | bytes 262176 | tf_op jit(solution)/shard_map/ppermute | solution.py:68
  39.3 11.9 %collective-permute-done.1.refs_2_ = bf16[128,1024]{1,0:T(8,128)(2,1)S(1)} collective-permute-done((bf16[128,1024]{1,0:T(8,128)(2,1)S(1)}, bf16[128,1024]{1,0:T(8,128)(2,1)S(1)}, u32[]{:S(2)}, u32[]{:S(2)}) %collective-permute-start.1) | collective-permute-done | bytes 262176 | tf_op jit(solution)/shard_map/ppermute | solution.py:68
  51.2 0.0 collective-permute-done.5.refs_4_
  51.2 1.4 %project.1 = (bf16[384,1024]{1,0:T(8,128)(2,1)}, bf16[512,384]{1,0:T(8,128)(2,1)}, bf16[384,1024]{1,0:T(8,128)(2,1)S(1)}) custom-call(bf16[128,1024]{1,0:T(8,128)(2,1)S(1)} %get-tuple-element.9.refs_0_, bf16[128,1024]{1,0:T(8,128)(2,1)S(1)} %collective-permute-done.refs_1_, bf16[128,1024]{1,0:T(8,128)(2,1)S(1)} %collective-permute-done.1.refs_2_, ...), custom_call_target="tpu_custom_call" | custom-call | flops 301989888 | bytes 3440640 | tf_op jit(solution)/shard_map/project/pallas_call | solution.py:242
  52.5 0.0 collective-permute-done.6.block_ref
  52.6 1.0 %last.1 = bf16[512,384]{1,0:T(8,128)(2,1)} custom-call(bf16[128,1024]{1,0:T(8,128)(2,1)S(1)} %collective-permute-done.6.block_ref, bf16[384,1024]{1,0:T(8,128)(2,1)S(1)} %get-tuple-element.14.weight_ref, bf16[512,384]{1,0:T(8,128)(2,1)} %get-tuple-element.15._), custom_call_target="tpu_custom_call", output_to_operand_aliasing={{}: (2, {})} | custom-call | flops 100663296 | bytes 360448 | tf_op jit(solution)/shard_map/last/pallas_call | solution.py:264
  (4 shorter events, 0.0 us)
Async XLA Ops:
  1.6 15.0 %collective-permute-start.2 = (bf16[96,1024]{1,0:T(8,128)(2,1)S(1)}, bf16[96,1024]{1,0:T(8,128)(2,1)S(1)}, u32[]{:S(2)}, u32[]{:S(2)}) collective-permute-start(bf16[96,1024]{1,0:T(8,128)(2,1)S(1)} %slice.5), channel_id=1, source_target_pairs={{0,3},{1,2},{2,0},{3,1},{4,7},{5,6},{6,4},{7,5},{8,11},{9,10},{10,... | collective-permute-start | bytes 589832 | tf_op jit(solution)/shard_map/ppermute | solution.py:68
  7.7 13.7 %copy-start = (bf16[1,1,384,1024]{3,2,1,0:T(8,128)(2,1)S(1)}, bf16[1,1,384,1024]{3,2,1,0:T(8,128)(2,1)}, u32[]{:S(2)}) copy-start(bf16[1,1,384,1024]{3,2,1,0:T(8,128)(2,1)} %param.5) | copy-start | bytes 2359300
  7.7 13.7 %collective-permute-start.3 = (bf16[96,1024]{1,0:T(8,128)(2,1)S(1)}, bf16[96,1024]{1,0:T(8,128)(2,1)S(1)}, u32[]{:S(2)}, u32[]{:S(2)}) collective-permute-start(bf16[96,1024]{1,0:T(8,128)(2,1)S(1)} %slice.6), channel_id=1, source_target_pairs={{0,1},{1,0},{2,3},{3,2},{4,5},{5,4},{6,7},{7,6},{8,9},{9,8},{10,11... | collective-permute-start | bytes 589832 | tf_op jit(solution)/shard_map/ppermute | solution.py:68
  8.8 12.6 %collective-permute-start.4 = (bf16[96,1024]{1,0:T(8,128)(2,1)S(1)}, bf16[96,1024]{1,0:T(8,128)(2,1)S(1)}, u32[]{:S(2)}, u32[]{:S(2)}) collective-permute-start(bf16[96,1024]{1,0:T(8,128)(2,1)S(1)} %slice.7), channel_id=1, source_target_pairs={{0,2},{1,3},{2,1},{3,0},{4,6},{5,7},{6,5},{7,4},{8,10},{9,11},{10,... | collective-permute-start | bytes 589832 | tf_op jit(solution)/shard_map/ppermute | solution.py:68
  21.4 4.3 %copy-start.1 = (bf16[1,256,1024]{2,1,0:T(8,128)(2,1)S(1)}, bf16[1,256,1024]{2,1,0:T(8,128)(2,1)}, u32[]{:S(2)}) copy-start(bf16[1,256,1024]{2,1,0:T(8,128)(2,1)} %param.6) | copy-start | bytes 1572868
  24.0 27.2 %collective-permute-start.5 = (bf16[384,1024]{1,0:T(8,128)(2,1)S(1)}, bf16[384,1024]{1,0:T(8,128)(2,1)S(1)}, u32[]{:S(2)}, u32[]{:S(2)}) collective-permute-start(bf16[384,1024]{1,0:T(8,128)(2,1)S(1)} %update.1.refs_3_), channel_id=1, source_target_pairs={{0,16},{4,20},{8,24},{12,28},{16,0},{20,4},{24,8},{28,12},{1,17},{... | collective-permute-start | bytes 2359304 | tf_op jit(solution)/shard_map/ppermute | solution.py:235
  25.6 0.7 %copy-start.2 = (s32[1,256,1]{1,2,0:T(1,128)S(1)}, s32[1,256,1]{1,2,0:T(1,128)}, u32[]{:S(2)}) copy-start(s32[1,256,1]{1,2,0:T(1,128)} %param.7) | copy-start | bytes 3076
  27.3 11.9 %collective-permute-start = (bf16[128,1024]{1,0:T(8,128)(2,1)S(1)}, bf16[128,1024]{1,0:T(8,128)(2,1)S(1)}, u32[]{:S(2)}, u32[]{:S(2)}) collective-permute-start(bf16[128,1024]{1,0:T(8,128)(2,1)S(1)} %get-tuple-element.10), channel_id=1, source_target_pairs={{0,1},{1,0},{2,3},{3,2},{4,5},{5,4},{6,7},{7,6},{8,9},{9,8},{10,11... | collective-permute-start | bytes 786440 | tf_op jit(solution)/shard_map/ppermute | solution.py:68
  29.9 21.3 %collective-permute-start.1 = (bf16[128,1024]{1,0:T(8,128)(2,1)S(1)}, bf16[128,1024]{1,0:T(8,128)(2,1)S(1)}, u32[]{:S(2)}, u32[]{:S(2)}) collective-permute-start(bf16[128,1024]{1,0:T(8,128)(2,1)S(1)} %get-tuple-element.11), channel_id=1, source_target_pairs={{0,2},{1,3},{2,0},{3,1},{4,6},{5,7},{6,4},{7,5},{8,10},{9,11},{10,... | collective-permute-start | bytes 786440 | tf_op jit(solution)/shard_map/ppermute | solution.py:68
  32.4 20.1 %collective-permute-start.6 = (bf16[128,1024]{1,0:T(8,128)(2,1)S(1)}, bf16[128,1024]{1,0:T(8,128)(2,1)S(1)}, u32[]{:S(2)}, u32[]{:S(2)}) collective-permute-start(bf16[128,1024]{1,0:T(8,128)(2,1)S(1)} %get-tuple-element.13), channel_id=1, source_target_pairs={{0,3},{1,2},{2,1},{3,0},{4,7},{5,6},{6,5},{7,4},{8,11},{9,10},{10,... | collective-permute-start | bytes 786440 | tf_op jit(solution)/shard_map/ppermute | solution.py:68

commit v3 on v2

--- a/solution.py
+++ b/solution.py
@@ -18,7 +18,7 @@
 coef_c = 2.0315
 step_rate = 0.5
 MH = ("c3", 1, "c1")
-TH = (1, 2, 3)
+TH = (1, "c3", "c1")
 STEPS = {
     1: (1, 0, 3, 2),
     2: (2, 3, 0, 1),
@@ -139,7 +139,7 @@
 def project_kernel(come, width, *refs):
     nodes = len(come)
     blocks, own_ref, partner_ref = refs[:nodes], refs[nodes], refs[nodes + 1]
-    weight_out, rows_out, weight_ref, slot_ref, rows_ref, sems = refs[nodes + 2 :]
+    weight_out, rows_out, turned_ref, weight_ref, slot_ref, rows_ref, sems = refs[nodes + 2 :]
     me = lax.axis_index("fsdp")
     capacity = blocks[0].shape[0]
     weight = (
@@ -159,14 +159,15 @@
             )
         )
         copies[-1].start()
+    turned_ref[...] = weight.T
     for cp in copies:
         cp.wait()
 
 
-def last_kernel(come, width, block_ref, weight_ref, _, rows_out, rows_ref, sem):
+def last_kernel(come, width, block_ref, turned_ref, _, rows_out, rows_ref, sem):
     me = lax.axis_index("fsdp")
     capacity = block_ref.shape[0]
-    rows_ref[...] = (dot_t(block_ref[...], weight_ref[...]) * (1.0 / math.sqrt(width))).astype(
+    rows_ref[...] = (dot(block_ref[...], turned_ref[...]) * (1.0 / math.sqrt(width))).astype(
         jnp.bfloat16
     )
     home = pl.ds(pl.multiple_of(at(come, me) * capacity, capacity), capacity)
@@ -244,11 +245,12 @@
         out_shape=(
             jax.ShapeDtypeStruct((total, width), jnp.bfloat16),
             rows_shape,
-            jax.ShapeDtypeStruct((total, width), jnp.bfloat16),
+            jax.ShapeDtypeStruct((width, total), jnp.bfloat16),
         ),
         in_specs=[VMEM] * (early + 2),
         out_specs=(hbm, hbm, VMEM),
         scratch_shapes=[
+            pltpu.VMEM((total, width), jnp.bfloat16),
             pltpu.VMEM((early * capacity, width), jnp.bfloat16),
             pltpu.VMEM((early * capacity, total), jnp.bfloat16),
             pltpu.SemaphoreType.DMA((nodes,)),

time: 53.8 us -> 53.7 us (level)
  no operation moved by 1% of the time
where the time goes in v3:
time: 53.7 us; the launch traced here: 53.5 us
  waiting for transfers between devices  29.2 us (54%)
  starting transfers between devices  13.2 us (25%)
  Pallas kernels  9.75 us (18%)
  between operations  0.72 us (1%)
  local copies, waits for them, and re-layouts  0.69 us (1%)
    ppermute x6, waiting for transfers between devices, trade(): return lax.ppermute(block, 'fsdp', list(enumerate(step)))  29.2 us
    ppermute x6, starting transfers between devices, trade(): return lax.ppermute(block, 'fsdp', list(enumerate(step)))  11.5 us
    pallas_call x4, Pallas kernels, per_device(): pl.pallas_call(functools.partial(slice_kernel, step), out_shape=jax.Shape...  3.82 us
    pallas_call x1, Pallas kernels, per_device(): pl.pallas_call(functools.partial(update_kernel, [inverse(s) for s in far]...  2.62 us
    ppermute x1, starting transfers between devices, per_device(): lax.ppermute(updated, 'replica', [(i, i ^ 1 << GOSSIP_BIT) for i in range...  1.63 us
    pallas_call x1, Pallas kernels, per_device(): pl.pallas_call(functools.partial(project_kernel, come[:early], width), ou...  1.36 us
  transfers between devices with their start and end apart: 7, of which 4 were waited for; matrix products, arithmetic and copies ran while one was open for 0% of the time, Pallas kernels for 10%

profile of v3, /device:TPU:0, one launch (start us, length us, event | category | flops | bytes accessed | tf_op | source)
XLA Modules:
  0.0 53.5 jit_solution(4613520589741431940)
XLA Ops:
  0.6 0.9 %slice.5 = bf16[96,1024]{1,0:T(8,128)(2,1)S(1)} custom-call(bf16[4,96,1024]{2,1,0:T(8,128)(2,1)} %bitcast.9), custom_call_target="tpu_custom_call" | custom-call | tf_op jit(solution)/shard_map/slice/pallas_call | solution.py:192
  1.6 5.1 %collective-permute-start.2 = (bf16[96,1024]{1,0:T(8,128)(2,1)S(1)}, bf16[96,1024]{1,0:T(8,128)(2,1)S(1)}, u32[]{:S(2)}, u32[]{:S(2)}) collective-permute-start(bf16[96,1024]{1,0:T(8,128)(2,1)S(1)} %slice.5), channel_id=1, source_target_pairs={{0,3},{1,2},{2,0},{3,1},{4,7},{5,6},{6,4},{7,5},{8,11},{9,10},{10,... | collective-permute-start | bytes 589832 | tf_op jit(solution)/shard_map/ppermute | solution.py:68
  6.7 0.9 %slice.6 = bf16[96,1024]{1,0:T(8,128)(2,1)S(1)} custom-call(bf16[4,96,1024]{2,1,0:T(8,128)(2,1)} %bitcast.10), custom_call_target="tpu_custom_call" | custom-call | tf_op jit(solution)/shard_map/slice/pallas_call | solution.py:192
  7.7 0.0 copy-start
  7.7 0.1 collective-permute-start.3
  7.7 1.0 %slice.7 = bf16[96,1024]{1,0:T(8,128)(2,1)S(1)} custom-call(bf16[4,96,1024]{2,1,0:T(8,128)(2,1)} %bitcast.11), custom_call_target="tpu_custom_call" | custom-call | tf_op jit(solution)/shard_map/slice/pallas_call | solution.py:192
  8.8 0.9 %collective-permute-start.4 = (bf16[96,1024]{1,0:T(8,128)(2,1)S(1)}, bf16[96,1024]{1,0:T(8,128)(2,1)S(1)}, u32[]{:S(2)}, u32[]{:S(2)}) collective-permute-start(bf16[96,1024]{1,0:T(8,128)(2,1)S(1)} %slice.7), channel_id=1, source_target_pairs={{0,2},{1,3},{2,1},{3,0},{4,6},{5,7},{6,5},{7,4},{8,10},{9,11},{10,... | collective-permute-start | bytes 589832 | tf_op jit(solution)/shard_map/ppermute | solution.py:68
  9.6 0.9 %slice.4.refs_0_ = bf16[96,1024]{1,0:T(8,128)(2,1)S(1)} custom-call(bf16[4,96,1024]{2,1,0:T(8,128)(2,1)} %bitcast.12), custom_call_target="tpu_custom_call" | custom-call | tf_op jit(solution)/shard_map/slice/pallas_call | solution.py:192
  10.6 6.0 %collective-permute-done.2.refs_1_ = bf16[96,1024]{1,0:T(8,128)(2,1)S(1)} collective-permute-done((bf16[96,1024]{1,0:T(8,128)(2,1)S(1)}, bf16[96,1024]{1,0:T(8,128)(2,1)S(1)}, u32[]{:S(2)}, u32[]{:S(2)}) %collective-permute-start.2) | collective-permute-done | bytes 196640 | tf_op jit(solution)/shard_map/ppermute | solution.py:68
  16.6 4.8 %collective-permute-done.3.refs_2_ = bf16[96,1024]{1,0:T(8,128)(2,1)S(1)} collective-permute-done((bf16[96,1024]{1,0:T(8,128)(2,1)S(1)}, bf16[96,1024]{1,0:T(8,128)(2,1)S(1)}, u32[]{:S(2)}, u32[]{:S(2)}) %collective-permute-start.3) | collective-permute-done | bytes 196640 | tf_op jit(solution)/shard_map/ppermute | solution.py:68
  21.4 0.0 collective-permute-done.4.refs_3_
  21.4 2.6 %update.1.refs_3_ = bf16[384,1024]{1,0:T(8,128)(2,1)S(1)} custom-call(bf16[96,1024]{1,0:T(8,128)(2,1)S(1)} %slice.4.refs_0_, bf16[96,1024]{1,0:T(8,128)(2,1)S(1)} %collective-permute-done.2.refs_1_, bf16[96,1024]{1,0:T(8,128)(2,1)S(1)} %collective-permute-done.3.refs_2_, bf16[96,1024]{1,0:T(8,128)(2,1)S(1)} %collective-permute-done.4.refs_3_, ...), custom_call_target="tpu_custom_call" | custom-call | flops 1170210816 | bytes 2359296 | tf_op jit(solution)/shard_map/update/pallas_call | solution.py:222
  24.0 1.6 %collective-permute-start.5 = (bf16[384,1024]{1,0:T(8,128)(2,1)S(1)}, bf16[384,1024]{1,0:T(8,128)(2,1)S(1)}, u32[]{:S(2)}, u32[]{:S(2)}) collective-permute-start(bf16[384,1024]{1,0:T(8,128)(2,1)S(1)} %update.1.refs_3_), channel_id=1, source_target_pairs={{0,16},{4,20},{8,24},{12,28},{16,0},{20,4},{24,8},{28,12},{1,17},{... | collective-permute-start | bytes 2359304 | tf_op jit(solution)/shard_map/ppermute | solution.py:236
  25.6 0.7 %copy-done.2 = s32[1,256,1]{1,2,0:T(1,128)S(1)} copy-done((s32[1,256,1]{1,2,0:T(1,128)S(1)}, s32[1,256,1]{1,2,0:T(1,128)}, u32[]{:S(2)}) %copy-start.2) | copy-done | bytes 1048
  26.3 1.0 %pack.1 = (bf16[128,1024]{1,0:T(8,128)(2,1)S(1)}, bf16[128,1024]{1,0:T(8,128)(2,1)S(1)}, bf16[128,1024]{1,0:T(8,128)(2,1)S(1)}, bf16[128,1024]{1,0:T(8,128)(2,1)S(1)}) custom-call(s32[1,256]{1,0:T(1,128)S(1)} %bitcast.8, bf16[256,1024]{1,0:T(8,128)(2,1)S(1)} %bitcast.7), custom_call_target="tpu_custom_call" | custom-call | flops 268435456 | bytes 1572864 | tf_op jit(solution)/shard_map/pack/pallas_call | solution.py:204
  27.3 2.5 %collective-permute-start = (bf16[128,1024]{1,0:T(8,128)(2,1)S(1)}, bf16[128,1024]{1,0:T(8,128)(2,1)S(1)}, u32[]{:S(2)}, u32[]{:S(2)}) collective-permute-start(bf16[128,1024]{1,0:T(8,128)(2,1)S(1)} %get-tuple-element.10), channel_id=1, source_target_pairs={{0,1},{1,0},{2,3},{3,2},{4,5},{5,4},{6,7},{7,6},{8,9},{9,8},{10,11... | collective-permute-start | bytes 786440 | tf_op jit(solution)/shard_map/ppermute | solution.py:68
  29.9 2.1 %collective-permute-start.1 = (bf16[128,1024]{1,0:T(8,128)(2,1)S(1)}, bf16[128,1024]{1,0:T(8,128)(2,1)S(1)}, u32[]{:S(2)}, u32[]{:S(2)}) collective-permute-start(bf16[128,1024]{1,0:T(8,128)(2,1)S(1)} %get-tuple-element.11), channel_id=1, source_target_pairs={{0,3},{1,2},{2,0},{3,1},{4,7},{5,6},{6,4},{7,5},{8,11},{9,10},{10,... | collective-permute-start | bytes 786440 | tf_op jit(solution)/shard_map/ppermute | solution.py:68
  31.9 0.9 %collective-permute-start.6 = (bf16[128,1024]{1,0:T(8,128)(2,1)S(1)}, bf16[128,1024]{1,0:T(8,128)(2,1)S(1)}, u32[]{:S(2)}, u32[]{:S(2)}) collective-permute-start(bf16[128,1024]{1,0:T(8,128)(2,1)S(1)} %get-tuple-element.13), channel_id=1, source_target_pairs={{0,2},{1,3},{2,1},{3,0},{4,6},{5,7},{6,5},{7,4},{8,10},{9,11},{10,... | collective-permute-start | bytes 786440 | tf_op jit(solution)/shard_map/ppermute | solution.py:68
  32.8 6.5 %collective-permute-done.refs_1_ = bf16[128,1024]{1,0:T(8,128)(2,1)S(1)} collective-permute-done((bf16[128,1024]{1,0:T(8,128)(2,1)S(1)}, bf16[128,1024]{1,0:T(8,128)(2,1)S(1)}, u32[]{:S(2)}, u32[]{:S(2)}) %collective-permute-start) | collective-permute-done | bytes 262176 | tf_op jit(solution)/shard_map/ppermute | solution.py:68
  39.3 11.9 %collective-permute-done.1.refs_2_ = bf16[128,1024]{1,0:T(8,128)(2,1)S(1)} collective-permute-done((bf16[128,1024]{1,0:T(8,128)(2,1)S(1)}, bf16[128,1024]{1,0:T(8,128)(2,1)S(1)}, u32[]{:S(2)}, u32[]{:S(2)}) %collective-permute-start.1) | collective-permute-done | bytes 262176 | tf_op jit(solution)/shard_map/ppermute | solution.py:68
  51.2 0.0 collective-permute-done.5.refs_4_
  51.2 1.4 %project.1 = (bf16[384,1024]{1,0:T(8,128)(2,1)}, bf16[512,384]{1,0:T(8,128)(2,1)}, bf16[1024,384]{1,0:T(8,128)(2,1)S(1)}) custom-call(bf16[128,1024]{1,0:T(8,128)(2,1)S(1)} %get-tuple-element.9.refs_0_, bf16[128,1024]{1,0:T(8,128)(2,1)S(1)} %collective-permute-done.refs_1_, bf16[128,1024]{1,0:T(8,128)(2,1)S(1)} %collective-permute-done.1.refs_2_, ...), custom_call_target="tpu_custom_call" | custom-call | flops 301989888 | bytes 3440640 | tf_op jit(solution)/shard_map/project/pallas_call | solution.py:243
  52.5 0.0 collective-permute-done.6.block_ref
  52.6 1.0 %last.1 = bf16[512,384]{1,0:T(8,128)(2,1)} custom-call(bf16[128,1024]{1,0:T(8,128)(2,1)S(1)} %collective-permute-done.6.block_ref, bf16[1024,384]{1,0:T(8,128)(2,1)S(1)} %get-tuple-element.14.turned_ref, bf16[512,384]{1,0:T(8,128)(2,1)} %get-tuple-element.15._), custom_call_target="tpu_custom_call", output_to_operand_aliasing={{}: (2, {})} | custom-call | flops 100663296 | bytes 360448 | tf_op jit(solution)/shard_map/last/pallas_call | solution.py:266
  (4 shorter events, 0.0 us)
Async XLA Ops:
  1.6 15.0 %collective-permute-start.2 = (bf16[96,1024]{1,0:T(8,128)(2,1)S(1)}, bf16[96,1024]{1,0:T(8,128)(2,1)S(1)}, u32[]{:S(2)}, u32[]{:S(2)}) collective-permute-start(bf16[96,1024]{1,0:T(8,128)(2,1)S(1)} %slice.5), channel_id=1, source_target_pairs={{0,3},{1,2},{2,0},{3,1},{4,7},{5,6},{6,4},{7,5},{8,11},{9,10},{10,... | collective-permute-start | bytes 589832 | tf_op jit(solution)/shard_map/ppermute | solution.py:68
  7.7 13.7 %copy-start = (bf16[1,1,384,1024]{3,2,1,0:T(8,128)(2,1)S(1)}, bf16[1,1,384,1024]{3,2,1,0:T(8,128)(2,1)}, u32[]{:S(2)}) copy-start(bf16[1,1,384,1024]{3,2,1,0:T(8,128)(2,1)} %param.5) | copy-start | bytes 2359300
  7.7 13.7 %collective-permute-start.3 = (bf16[96,1024]{1,0:T(8,128)(2,1)S(1)}, bf16[96,1024]{1,0:T(8,128)(2,1)S(1)}, u32[]{:S(2)}, u32[]{:S(2)}) collective-permute-start(bf16[96,1024]{1,0:T(8,128)(2,1)S(1)} %slice.6), channel_id=1, source_target_pairs={{0,1},{1,0},{2,3},{3,2},{4,5},{5,4},{6,7},{7,6},{8,9},{9,8},{10,11... | collective-permute-start | bytes 589832 | tf_op jit(solution)/shard_map/ppermute | solution.py:68
  8.8 12.6 %collective-permute-start.4 = (bf16[96,1024]{1,0:T(8,128)(2,1)S(1)}, bf16[96,1024]{1,0:T(8,128)(2,1)S(1)}, u32[]{:S(2)}, u32[]{:S(2)}) collective-permute-start(bf16[96,1024]{1,0:T(8,128)(2,1)S(1)} %slice.7), channel_id=1, source_target_pairs={{0,2},{1,3},{2,1},{3,0},{4,6},{5,7},{6,5},{7,4},{8,10},{9,11},{10,... | collective-permute-start | bytes 589832 | tf_op jit(solution)/shard_map/ppermute | solution.py:68
  21.4 4.3 %copy-start.1 = (bf16[1,256,1024]{2,1,0:T(8,128)(2,1)S(1)}, bf16[1,256,1024]{2,1,0:T(8,128)(2,1)}, u32[]{:S(2)}) copy-start(bf16[1,256,1024]{2,1,0:T(8,128)(2,1)} %param.6) | copy-start | bytes 1572868
  24.0 27.2 %collective-permute-start.5 = (bf16[384,1024]{1,0:T(8,128)(2,1)S(1)}, bf16[384,1024]{1,0:T(8,128)(2,1)S(1)}, u32[]{:S(2)}, u32[]{:S(2)}) collective-permute-start(bf16[384,1024]{1,0:T(8,128)(2,1)S(1)} %update.1.refs_3_), channel_id=1, source_target_pairs={{0,16},{4,20},{8,24},{12,28},{16,0},{20,4},{24,8},{28,12},{1,17},{... | collective-permute-start | bytes 2359304 | tf_op jit(solution)/shard_map/ppermute | solution.py:236
  25.6 0.7 %copy-start.2 = (s32[1,256,1]{1,2,0:T(1,128)S(1)}, s32[1,256,1]{1,2,0:T(1,128)}, u32[]{:S(2)}) copy-start(s32[1,256,1]{1,2,0:T(1,128)} %param.7) | copy-start | bytes 3076
  27.3 11.9 %collective-permute-start = (bf16[128,1024]{1,0:T(8,128)(2,1)S(1)}, bf16[128,1024]{1,0:T(8,128)(2,1)S(1)}, u32[]{:S(2)}, u32[]{:S(2)}) collective-permute-start(bf16[128,1024]{1,0:T(8,128)(2,1)S(1)} %get-tuple-element.10), channel_id=1, source_target_pairs={{0,1},{1,0},{2,3},{3,2},{4,5},{5,4},{6,7},{7,6},{8,9},{9,8},{10,11... | collective-permute-start | bytes 786440 | tf_op jit(solution)/shard_map/ppermute | solution.py:68
  29.9 21.3 %collective-permute-start.1 = (bf16[128,1024]{1,0:T(8,128)(2,1)S(1)}, bf16[128,1024]{1,0:T(8,128)(2,1)S(1)}, u32[]{:S(2)}, u32[]{:S(2)}) collective-permute-start(bf16[128,1024]{1,0:T(8,128)(2,1)S(1)} %get-tuple-element.11), channel_id=1, source_target_pairs={{0,3},{1,2},{2,0},{3,1},{4,7},{5,6},{6,4},{7,5},{8,11},{9,10},{10,... | collective-permute-start | bytes 786440 | tf_op jit(solution)/shard_map/ppermute | solution.py:68
  31.9 20.6 %collective-permute-start.6 = (bf16[128,1024]{1,0:T(8,128)(2,1)S(1)}, bf16[128,1024]{1,0:T(8,128)(2,1)S(1)}, u32[]{:S(2)}, u32[]{:S(2)}) collective-permute-start(bf16[128,1024]{1,0:T(8,128)(2,1)S(1)} %get-tuple-element.13), channel_id=1, source_target_pairs={{0,2},{1,3},{2,1},{3,0},{4,6},{5,7},{6,5},{7,4},{8,10},{9,11},{10,... | collective-permute-start | bytes 786440 | tf_op jit(solution)/shard_map/ppermute | solution.py:68

commit v4 on v3

--- a/solution.py
+++ b/solution.py
@@ -17,8 +17,8 @@
 coef_b = -4.775
 coef_c = 2.0315
 step_rate = 0.5
-MH = ("c3", 1, "c1")
-TH = (1, "c3", "c1")
+MH = (("b3", "b1", 3), ("c3", 1, "c1"))
+TH = ((1, "c3", "c1"), (1, "c3", "c1"))
 STEPS = {
     1: (1, 0, 3, 2),
     2: (2, 3, 0, 1),
@@ -50,11 +50,11 @@
     return [tuple((i + k) % nodes for i in range(nodes)) for k in (*range(2, nodes), 1)]
 
 
-def inverse(step):
-    return tuple(step.index(i) for i in range(len(step)))
-
-
-def at(step, me):
+def inverse(pair):
+    return tuple(tuple(step.index(i) for i in range(len(step))) for step in pair)
+
+
+def entry(step, me):
     hop = step[0]
     if all(to == i ^ hop for i, to in enumerate(step)):
         return me ^ hop
@@ -64,8 +64,21 @@
     return found
 
 
-def trade(block, step):
-    return lax.ppermute(block, "fsdp", list(enumerate(step)))
+def at(pair, me):
+    even, odd = pair
+    if even == odd:
+        return entry(even, me)
+    return jnp.where(lax.axis_index("replica") % 2 == 0, entry(even, me), entry(odd, me))
+
+
+def trade(block, pair):
+    nodes = len(pair[0])
+    pairs = [
+        (r * nodes + i, r * nodes + to)
+        for r in range(lax.axis_size("replica"))
+        for i, to in enumerate(pair[r % 2])
+    ]
+    return lax.ppermute(block, ("replica", "fsdp"), pairs)
 
 
 def slice_kernel(step, source_ref, out_ref, sem):
@@ -182,9 +195,9 @@
     total = weights.shape[2]
     tok_rows = tokens.shape[1]
     capacity = 2 * tok_rows // nodes
-    here = tuple(range(nodes))
-    far = [here, *steps(nodes, MH)]
-    near = [here, *steps(nodes, TH)]
+    here = (tuple(range(nodes)),) * 2
+    far = [here, *zip(*(steps(nodes, order) for order in MH))]
+    near = [here, *zip(*(steps(nodes, order) for order in TH))]
 
     source = pltpu.with_memory_space_constraint(momentum[0], pltpu.HBM)
     blocks = []

time: 53.7 us -> 52.8 us (0.983)
  waiting for transfers between devices: 29.2 us -> 26.1 us
  starting transfers between devices: 13.2 us -> 15.2 us
    ppermute x6, waiting for transfers between devices: 29.2 us -> 26.1 us  [trade(): return lax.ppermute(block, ('replica', 'fsdp'), pairs)]
    ppermute x6, starting transfers between devices: 11.5 us -> 13.6 us  [trade(): return lax.ppermute(block, ('replica', 'fsdp'), pairs)]
  transfers between devices with their start and end apart: 7 -> 7, of which waited for: 4 -> 3; matrix products, arithmetic and copies ran while one was open for 0% -> 0% of each run, Pallas kernels for 10% -> 10%
where the time goes in v4:
time: 52.8 us; the launch traced here: 52.5 us
  waiting for transfers between devices  26.1 us (49%)
  starting transfers between devices  15.2 us (29%)
  Pallas kernels  9.76 us (18%)
  between operations  0.72 us (1%)
  local copies, waits for them, and re-layouts  0.69 us (1%)
    ppermute x6, waiting for transfers between devices, trade(): return lax.ppermute(block, ('replica', 'fsdp'), pairs)  26.1 us
    ppermute x6, starting transfers between devices, trade(): return lax.ppermute(block, ('replica', 'fsdp'), pairs)  13.6 us
    pallas_call x4, Pallas kernels, per_device(): pl.pallas_call(functools.partial(slice_kernel, step), out_shape=jax.Shape...  3.83 us
    pallas_call x1, Pallas kernels, per_device(): pl.pallas_call(functools.partial(update_kernel, [inverse(s) for s in far]...  2.62 us
    ppermute x1, starting transfers between devices, per_device(): lax.ppermute(updated, 'replica', [(i, i ^ 1 << GOSSIP_BIT) for i in range...  1.58 us
    pallas_call x1, Pallas kernels, per_device(): pl.pallas_call(functools.partial(project_kernel, come[:early], width), ou...  1.36 us
  transfers between devices with their start and end apart: 7, of which 3 were waited for; matrix products, arithmetic and copies ran while one was open for 0% of the time, Pallas kernels for 10%

profile of v4, /device:TPU:0, one launch (start us, length us, event | category | flops | bytes accessed | tf_op | source)
XLA Modules:
  0.0 52.5 jit_solution(13443524634425544907)
XLA Ops:
  0.6 1.0 %slice.5 = bf16[96,1024]{1,0:T(8,128)(2,1)S(1)} custom-call(bf16[4,96,1024]{2,1,0:T(8,128)(2,1)} %bitcast.9), custom_call_target="tpu_custom_call" | custom-call | tf_op jit(solution)/shard_map/slice/pallas_call | solution.py:205
  1.6 4.1 %collective-permute-start.2 = (bf16[96,1024]{1,0:T(8,128)(2,1)S(1)}, bf16[96,1024]{1,0:T(8,128)(2,1)S(1)}, u32[]{:S(2)}, u32[]{:S(2)}) collective-permute-start(bf16[96,1024]{1,0:T(8,128)(2,1)S(1)} %slice.5), channel_id=1, source_target_pairs={{0,2},{1,0},{2,3},{3,1},{4,7},{5,6},{6,4},{7,5},{8,10},{9,8},{10,1... | collective-permute-start | bytes 589832 | tf_op jit(solution)/shard_map/ppermute | solution.py:81
  5.7 0.9 %slice.6 = bf16[96,1024]{1,0:T(8,128)(2,1)S(1)} custom-call(bf16[4,96,1024]{2,1,0:T(8,128)(2,1)} %bitcast.10), custom_call_target="tpu_custom_call" | custom-call | tf_op jit(solution)/shard_map/slice/pallas_call | solution.py:205
  6.6 0.0 copy-start
  6.7 0.1 collective-permute-start.3
  6.7 1.0 %slice.7 = bf16[96,1024]{1,0:T(8,128)(2,1)S(1)} custom-call(bf16[4,96,1024]{2,1,0:T(8,128)(2,1)} %bitcast.11), custom_call_target="tpu_custom_call" | custom-call | tf_op jit(solution)/shard_map/slice/pallas_call | solution.py:205
  7.7 3.0 %collective-permute-start.4 = (bf16[96,1024]{1,0:T(8,128)(2,1)S(1)}, bf16[96,1024]{1,0:T(8,128)(2,1)S(1)}, u32[]{:S(2)}, u32[]{:S(2)}) collective-permute-start(bf16[96,1024]{1,0:T(8,128)(2,1)S(1)} %slice.7), channel_id=1, source_target_pairs={{0,3},{1,2},{2,1},{3,0},{4,6},{5,7},{6,5},{7,4},{8,11},{9,10},{10,... | collective-permute-start | bytes 589832 | tf_op jit(solution)/shard_map/ppermute | solution.py:81
  10.7 0.9 %slice.4.refs_0_ = bf16[96,1024]{1,0:T(8,128)(2,1)S(1)} custom-call(bf16[4,96,1024]{2,1,0:T(8,128)(2,1)} %bitcast.12), custom_call_target="tpu_custom_call" | custom-call | tf_op jit(solution)/shard_map/slice/pallas_call | solution.py:205
  11.7 0.0 collective-permute-done.2.refs_1_
  11.7 8.7 %collective-permute-done.3.refs_2_ = bf16[96,1024]{1,0:T(8,128)(2,1)S(1)} collective-permute-done((bf16[96,1024]{1,0:T(8,128)(2,1)S(1)}, bf16[96,1024]{1,0:T(8,128)(2,1)S(1)}, u32[]{:S(2)}, u32[]{:S(2)}) %collective-permute-start.3) | collective-permute-done | bytes 196640 | tf_op jit(solution)/shard_map/ppermute | solution.py:81
  20.4 0.0 collective-permute-done.4.refs_3_
  20.4 2.6 %update.1.refs_3_ = bf16[384,1024]{1,0:T(8,128)(2,1)S(1)} custom-call(bf16[96,1024]{1,0:T(8,128)(2,1)S(1)} %slice.4.refs_0_, bf16[96,1024]{1,0:T(8,128)(2,1)S(1)} %collective-permute-done.2.refs_1_, bf16[96,1024]{1,0:T(8,128)(2,1)S(1)} %collective-permute-done.3.refs_2_, bf16[96,1024]{1,0:T(8,128)(2,1)S(1)} %collective-permute-done.4.refs_3_, ...), custom_call_target="tpu_custom_call" | custom-call | flops 1170210816 | bytes 2359296 | tf_op jit(solution)/shard_map/update/pallas_call | solution.py:235
  23.0 1.6 %collective-permute-start.5 = (bf16[384,1024]{1,0:T(8,128)(2,1)S(1)}, bf16[384,1024]{1,0:T(8,128)(2,1)S(1)}, u32[]{:S(2)}, u32[]{:S(2)}) collective-permute-start(bf16[384,1024]{1,0:T(8,128)(2,1)S(1)} %update.1.refs_3_), channel_id=1, source_target_pairs={{0,16},{4,20},{8,24},{12,28},{16,0},{20,4},{24,8},{28,12},{1,17},{... | collective-permute-start | bytes 2359304 | tf_op jit(solution)/shard_map/ppermute | solution.py:249
  24.6 0.7 %copy-done.2 = s32[1,256,1]{1,2,0:T(1,128)S(1)} copy-done((s32[1,256,1]{1,2,0:T(1,128)S(1)}, s32[1,256,1]{1,2,0:T(1,128)}, u32[]{:S(2)}) %copy-start.2) | copy-done | bytes 1048
  25.3 1.0 %pack.1 = (bf16[128,1024]{1,0:T(8,128)(2,1)S(1)}, bf16[128,1024]{1,0:T(8,128)(2,1)S(1)}, bf16[128,1024]{1,0:T(8,128)(2,1)S(1)}, bf16[128,1024]{1,0:T(8,128)(2,1)S(1)}) custom-call(s32[1,256]{1,0:T(1,128)S(1)} %bitcast.8, bf16[256,1024]{1,0:T(8,128)(2,1)S(1)} %bitcast.7), custom_call_target="tpu_custom_call" | custom-call | flops 268435456 | bytes 1572864 | tf_op jit(solution)/shard_map/pack/pallas_call | solution.py:217
  26.3 3.5 %collective-permute-start = (bf16[128,1024]{1,0:T(8,128)(2,1)S(1)}, bf16[128,1024]{1,0:T(8,128)(2,1)S(1)}, u32[]{:S(2)}, u32[]{:S(2)}) collective-permute-start(bf16[128,1024]{1,0:T(8,128)(2,1)S(1)} %get-tuple-element.10), channel_id=1, source_target_pairs={{0,1},{1,0},{2,3},{3,2},{4,5},{5,4},{6,7},{7,6},{8,9},{9,8},{10,11... | collective-permute-start | bytes 786440 | tf_op jit(solution)/shard_map/ppermute | solution.py:81
  29.8 2.6 %collective-permute-start.1 = (bf16[128,1024]{1,0:T(8,128)(2,1)S(1)}, bf16[128,1024]{1,0:T(8,128)(2,1)S(1)}, u32[]{:S(2)}, u32[]{:S(2)}) collective-permute-start(bf16[128,1024]{1,0:T(8,128)(2,1)S(1)} %get-tuple-element.11), channel_id=1, source_target_pairs={{0,3},{1,2},{2,0},{3,1},{4,7},{5,6},{6,4},{7,5},{8,11},{9,10},{10,... | collective-permute-start | bytes 786440 | tf_op jit(solution)/shard_map/ppermute | solution.py:81
  32.4 0.3 collective-permute-start.6
  32.7 7.2 %collective-permute-done.refs_1_ = bf16[128,1024]{1,0:T(8,128)(2,1)S(1)} collective-permute-done((bf16[128,1024]{1,0:T(8,128)(2,1)S(1)}, bf16[128,1024]{1,0:T(8,128)(2,1)S(1)}, u32[]{:S(2)}, u32[]{:S(2)}) %collective-permute-start) | collective-permute-done | bytes 262176 | tf_op jit(solution)/shard_map/ppermute | solution.py:81
  39.9 10.3 %collective-permute-done.1.refs_2_ = bf16[128,1024]{1,0:T(8,128)(2,1)S(1)} collective-permute-done((bf16[128,1024]{1,0:T(8,128)(2,1)S(1)}, bf16[128,1024]{1,0:T(8,128)(2,1)S(1)}, u32[]{:S(2)}, u32[]{:S(2)}) %collective-permute-start.1) | collective-permute-done | bytes 262176 | tf_op jit(solution)/shard_map/ppermute | solution.py:81
  50.2 0.0 collective-permute-done.5.refs_4_
  50.2 1.4 %project.1 = (bf16[384,1024]{1,0:T(8,128)(2,1)}, bf16[512,384]{1,0:T(8,128)(2,1)}, bf16[1024,384]{1,0:T(8,128)(2,1)S(1)}) custom-call(bf16[128,1024]{1,0:T(8,128)(2,1)S(1)} %get-tuple-element.9.refs_0_, bf16[128,1024]{1,0:T(8,128)(2,1)S(1)} %collective-permute-done.refs_1_, bf16[128,1024]{1,0:T(8,128)(2,1)S(1)} %collective-permute-done.1.refs_2_, ...), custom_call_target="tpu_custom_call" | custom-call | flops 301989888 | bytes 3440640 | tf_op jit(solution)/shard_map/project/pallas_call | solution.py:256
  51.5 0.0 collective-permute-done.6.block_ref
  51.5 1.0 %last.1 = bf16[512,384]{1,0:T(8,128)(2,1)} custom-call(bf16[128,1024]{1,0:T(8,128)(2,1)S(1)} %collective-permute-done.6.block_ref, bf16[1024,384]{1,0:T(8,128)(2,1)S(1)} %get-tuple-element.14.turned_ref, bf16[512,384]{1,0:T(8,128)(2,1)} %get-tuple-element.15._), custom_call_target="tpu_custom_call", output_to_operand_aliasing={{}: (2, {})} | custom-call | flops 100663296 | bytes 360448 | tf_op jit(solution)/shard_map/last/pallas_call | solution.py:279
  (4 shorter events, 0.0 us)
Async XLA Ops:
  1.6 10.1 %collective-permute-start.2 = (bf16[96,1024]{1,0:T(8,128)(2,1)S(1)}, bf16[96,1024]{1,0:T(8,128)(2,1)S(1)}, u32[]{:S(2)}, u32[]{:S(2)}) collective-permute-start(bf16[96,1024]{1,0:T(8,128)(2,1)S(1)} %slice.5), channel_id=1, source_target_pairs={{0,2},{1,0},{2,3},{3,1},{4,7},{5,6},{6,4},{7,5},{8,10},{9,8},{10,1... | collective-permute-start | bytes 589832 | tf_op jit(solution)/shard_map/ppermute | solution.py:81
  6.6 13.8 %copy-start = (bf16[1,1,384,1024]{3,2,1,0:T(8,128)(2,1)S(1)}, bf16[1,1,384,1024]{3,2,1,0:T(8,128)(2,1)}, u32[]{:S(2)}) copy-start(bf16[1,1,384,1024]{3,2,1,0:T(8,128)(2,1)} %param.5) | copy-start | bytes 2359300
  6.7 13.8 %collective-permute-start.3 = (bf16[96,1024]{1,0:T(8,128)(2,1)S(1)}, bf16[96,1024]{1,0:T(8,128)(2,1)S(1)}, u32[]{:S(2)}, u32[]{:S(2)}) collective-permute-start(bf16[96,1024]{1,0:T(8,128)(2,1)S(1)} %slice.6), channel_id=1, source_target_pairs={{0,1},{1,3},{2,0},{3,2},{4,5},{5,4},{6,7},{7,6},{8,9},{9,11},{10,8... | collective-permute-start | bytes 589832 | tf_op jit(solution)/shard_map/ppermute | solution.py:81
  7.7 12.7 %collective-permute-start.4 = (bf16[96,1024]{1,0:T(8,128)(2,1)S(1)}, bf16[96,1024]{1,0:T(8,128)(2,1)S(1)}, u32[]{:S(2)}, u32[]{:S(2)}) collective-permute-start(bf16[96,1024]{1,0:T(8,128)(2,1)S(1)} %slice.7), channel_id=1, source_target_pairs={{0,3},{1,2},{2,1},{3,0},{4,6},{5,7},{6,5},{7,4},{8,11},{9,10},{10,... | collective-permute-start | bytes 589832 | tf_op jit(solution)/shard_map/ppermute | solution.py:81
  20.4 4.2 %copy-start.1 = (bf16[1,256,1024]{2,1,0:T(8,128)(2,1)S(1)}, bf16[1,256,1024]{2,1,0:T(8,128)(2,1)}, u32[]{:S(2)}) copy-start(bf16[1,256,1024]{2,1,0:T(8,128)(2,1)} %param.6) | copy-start | bytes 1572868
  23.0 27.1 %collective-permute-start.5 = (bf16[384,1024]{1,0:T(8,128)(2,1)S(1)}, bf16[384,1024]{1,0:T(8,128)(2,1)S(1)}, u32[]{:S(2)}, u32[]{:S(2)}) collective-permute-start(bf16[384,1024]{1,0:T(8,128)(2,1)S(1)} %update.1.refs_3_), channel_id=1, source_target_pairs={{0,16},{4,20},{8,24},{12,28},{16,0},{20,4},{24,8},{28,12},{1,17},{... | collective-permute-start | bytes 2359304 | tf_op jit(solution)/shard_map/ppermute | solution.py:249
  24.6 0.7 %copy-start.2 = (s32[1,256,1]{1,2,0:T(1,128)S(1)}, s32[1,256,1]{1,2,0:T(1,128)}, u32[]{:S(2)}) copy-start(s32[1,256,1]{1,2,0:T(1,128)} %param.7) | copy-start | bytes 3076
  26.3 13.6 %collective-permute-start = (bf16[128,1024]{1,0:T(8,128)(2,1)S(1)}, bf16[128,1024]{1,0:T(8,128)(2,1)S(1)}, u32[]{:S(2)}, u32[]{:S(2)}) collective-permute-start(bf16[128,1024]{1,0:T(8,128)(2,1)S(1)} %get-tuple-element.10), channel_id=1, source_target_pairs={{0,1},{1,0},{2,3},{3,2},{4,5},{5,4},{6,7},{7,6},{8,9},{9,8},{10,11... | collective-permute-start | bytes 786440 | tf_op jit(solution)/shard_map/ppermute | solution.py:81
  29.8 20.3 %collective-permute-start.1 = (bf16[128,1024]{1,0:T(8,128)(2,1)S(1)}, bf16[128,1024]{1,0:T(8,128)(2,1)S(1)}, u32[]{:S(2)}, u32[]{:S(2)}) collective-permute-start(bf16[128,1024]{1,0:T(8,128)(2,1)S(1)} %get-tuple-element.11), channel_id=1, source_target_pairs={{0,3},{1,2},{2,0},{3,1},{4,7},{5,6},{6,4},{7,5},{8,11},{9,10},{10,... | collective-permute-start | bytes 786440 | tf_op jit(solution)/shard_map/ppermute | solution.py:81
  32.4 19.1 %collective-permute-start.6 = (bf16[128,1024]{1,0:T(8,128)(2,1)S(1)}, bf16[128,1024]{1,0:T(8,128)(2,1)S(1)}, u32[]{:S(2)}, u32[]{:S(2)}) collective-permute-start(bf16[128,1024]{1,0:T(8,128)(2,1)S(1)} %get-tuple-element.13), channel_id=1, source_target_pairs={{0,2},{1,3},{2,1},{3,0},{4,6},{5,7},{6,5},{7,4},{8,10},{9,11},{10,... | collective-permute-start | bytes 786440 | tf_op jit(solution)/shard_map/ppermute | solution.py:81

commit v5 on v4

--- a/solution.py
+++ b/solution.py
@@ -102,7 +102,13 @@
         count = dot(jnp.where(here, 1.0, 0.0).astype(jnp.bfloat16), earlier)
         position = jnp.where(here, count.astype(jnp.int32), -1)
         placing = jnp.where(slot == position, 1.0, 0.0).astype(jnp.bfloat16)
-        out_refs[k][...] = dot(placing, tokens).astype(jnp.bfloat16)
+        block = dot(placing, tokens).astype(jnp.bfloat16)
+        if k + 1 < len(to):
+            out_refs[k][...] = block
+        else:
+            cut = out_refs[k].shape[1]
+            out_refs[k][...] = block[:, :cut]
+            out_refs[k + 1][...] = block[:, cut:]
 
 
 def row_parts(rows):
@@ -151,7 +157,7 @@
 
 def project_kernel(come, width, *refs):
     nodes = len(come)
-    blocks, own_ref, partner_ref = refs[:nodes], refs[nodes], refs[nodes + 1]
+    blocks, own_ref, partner_ref = refs[:nodes], *refs[nodes : nodes + 2]
     weight_out, rows_out, turned_ref, weight_ref, slot_ref, rows_ref, sems = refs[nodes + 2 :]
     me = lax.axis_index("fsdp")
     capacity = blocks[0].shape[0]
@@ -177,12 +183,17 @@
         cp.wait()
 
 
-def last_kernel(come, width, block_ref, turned_ref, _, rows_out, rows_ref, sem):
+def part_kernel(block_ref, turned_ref, part_ref):
+    part_ref[...] = dot(block_ref[...], turned_ref[: block_ref.shape[1], :])
+
+
+def last_kernel(come, width, block_ref, turned_ref, part_ref, _, rows_out, rows_ref, sem):
     me = lax.axis_index("fsdp")
     capacity = block_ref.shape[0]
-    rows_ref[...] = (dot(block_ref[...], turned_ref[...]) * (1.0 / math.sqrt(width))).astype(
-        jnp.bfloat16
-    )
+    total = part_ref[...] + dot(
+        block_ref[...], turned_ref[turned_ref.shape[0] - block_ref.shape[1] :, :]
+    )
+    rows_ref[...] = (total * (1.0 / math.sqrt(width))).astype(jnp.bfloat16)
     home = pl.ds(pl.multiple_of(at(come, me) * capacity, capacity), capacity)
     cp = pltpu.make_async_copy(rows_ref, rows_out.at[home], sem)
     cp.start()
@@ -213,12 +224,16 @@
         )(source)
         blocks.append(trade(shard, step) if k else shard)
 
+    cut = width // 2
     packed = list(
         pl.pallas_call(
             functools.partial(pack_kernel, near, capacity),
-            out_shape=[jax.ShapeDtypeStruct((capacity, width), jnp.bfloat16)] * nodes,
+            out_shape=[
+                jax.ShapeDtypeStruct((capacity, columns), jnp.bfloat16)
+                for columns in (*[width] * (nodes - 1), cut, width - cut)
+            ],
             in_specs=[VMEM, VMEM],
-            out_specs=[VMEM] * nodes,
+            out_specs=[VMEM] * (nodes + 1),
             compiler_params=pltpu.CompilerParams(vmem_limit_bytes=16 << 20),
             cost_estimate=pl.CostEstimate(
                 flops=2 * nodes * capacity * tok_rows * width,
@@ -229,7 +244,7 @@
         )(routes.reshape(1, tok_rows), tokens[0])
     )
     slots = [packed[0]]
-    for k, step in enumerate(near[1:], 1):
+    for k, step in enumerate([*near[1:], near[-1]], 1):
         slots.append(trade(packed[k], step))
 
     updated = pl.pallas_call(
@@ -253,7 +268,7 @@
     early = nodes - 1
     rows_shape = jax.ShapeDtypeStruct((nodes * capacity, total), jnp.bfloat16)
     hbm = pl.BlockSpec(memory_space=pltpu.HBM)
-    averaged, expert_rows, kept = pl.pallas_call(
+    averaged, expert_rows, turned = pl.pallas_call(
         functools.partial(project_kernel, come[:early], width),
         out_shape=(
             jax.ShapeDtypeStruct((total, width), jnp.bfloat16),
@@ -276,16 +291,29 @@
         ),
         name="project",
     )(*slots[:early], updated, partner)
+    part = pl.pallas_call(
+        part_kernel,
+        out_shape=jax.ShapeDtypeStruct((capacity, total), jnp.float32),
+        in_specs=[VMEM, VMEM],
+        out_specs=VMEM,
+        compiler_params=pltpu.CompilerParams(vmem_limit_bytes=24 << 20),
+        cost_estimate=pl.CostEstimate(
+            flops=2 * capacity * cut * total,
+            bytes_accessed=2 * cut * (capacity + total),
+            transcendentals=0,
+        ),
+        name="part",
+    )(slots[early], turned)
     expert_rows = pl.pallas_call(
         functools.partial(last_kernel, come[early], width),
         out_shape=rows_shape,
-        in_specs=[VMEM, VMEM, hbm],
+        in_specs=[VMEM, VMEM, VMEM, hbm],
         out_specs=hbm,
         scratch_shapes=[
             pltpu.VMEM((capacity, total), jnp.bfloat16),
             pltpu.SemaphoreType.DMA,
         ],
-        input_output_aliases={2: 0},
+        input_output_aliases={3: 0},
         compiler_params=pltpu.CompilerParams(vmem_limit_bytes=24 << 20),
         cost_estimate=pl.CostEstimate(
             flops=2 * capacity * width * total,
@@ -293,7 +321,7 @@
             transcendentals=0,
         ),
         name="last",
-    )(slots[early], kept, expert_rows)
+    )(slots[early + 1], turned, part, expert_rows)
     return (averaged[None, None], expert_rows[None, None])
 
 

time: 52.8 us -> 52.9 us (level)
    ppermute x6 -> x7, starting transfers between devices: 13.6 us -> 13.9 us  [trade(): return lax.ppermute(block, ('replica', 'fsdp'), pairs)]
    ppermute x6 -> x7, waiting for transfers between devices: 26.1 us -> 25.8 us  [trade(): return lax.ppermute(block, ('replica', 'fsdp'), pairs)]
  transfers between devices with their start and end apart: 7 -> 8, of which waited for: 3 -> 3; matrix products, arithmetic and copies ran while one was open for 0% -> 0% of each run, Pallas kernels for 10% -> 10%
where the time goes in v5:
time: 52.9 us; the launch traced here: 52.7 us
  waiting for transfers between devices  25.8 us (49%)
  starting transfers between devices  15.5 us (29%)
  Pallas kernels  9.91 us (19%)
  between operations  0.74 us (1%)
  local copies, waits for them, and re-layouts  0.69 us (1%)
    ppermute x7, waiting for transfers between devices, trade(): return lax.ppermute(block, ('replica', 'fsdp'), pairs)  25.8 us
    ppermute x7, starting transfers between devices, trade(): return lax.ppermute(block, ('replica', 'fsdp'), pairs)  13.9 us
    pallas_call x4, Pallas kernels, per_device(): pl.pallas_call(functools.partial(slice_kernel, step), out_shape=jax.Shape...  3.83 us
    pallas_call x1, Pallas kernels, per_device(): pl.pallas_call(functools.partial(update_kernel, [inverse(s) for s in far]...  2.62 us
    ppermute x1, starting transfers between devices, per_device(): lax.ppermute(updated, 'replica', [(i, i ^ 1 << GOSSIP_BIT) for i in range...  1.58 us
    pallas_call x1, Pallas kernels, per_device(): pl.pallas_call(functools.partial(project_kernel, come[:early], width), ou...  1.36 us
  transfers between devices with their start and end apart: 8, of which 3 were waited for; matrix products, arithmetic and copies ran while one was open for 0% of the time, Pallas kernels for 10%

profile of v5, /device:TPU:0, one launch (start us, length us, event | category | flops | bytes accessed | tf_op | source)
XLA Modules:
  0.0 52.7 jit_solution(8377306873644419682)
XLA Ops:
  0.6 1.0 %slice.5 = bf16[96,1024]{1,0:T(8,128)(2,1)S(1)} custom-call(bf16[4,96,1024]{2,1,0:T(8,128)(2,1)} %bitcast.9), custom_call_target="tpu_custom_call" | custom-call | tf_op jit(solution)/shard_map/slice/pallas_call | solution.py:216
  1.6 4.1 %collective-permute-start.2 = (bf16[96,1024]{1,0:T(8,128)(2,1)S(1)}, bf16[96,1024]{1,0:T(8,128)(2,1)S(1)}, u32[]{:S(2)}, u32[]{:S(2)}) collective-permute-start(bf16[96,1024]{1,0:T(8,128)(2,1)S(1)} %slice.5), channel_id=1, source_target_pairs={{0,2},{1,0},{2,3},{3,1},{4,7},{5,6},{6,4},{7,5},{8,10},{9,8},{10,1... | collective-permute-start | bytes 589832 | tf_op jit(solution)/shard_map/ppermute | solution.py:81
  5.7 0.9 %slice.6 = bf16[96,1024]{1,0:T(8,128)(2,1)S(1)} custom-call(bf16[4,96,1024]{2,1,0:T(8,128)(2,1)} %bitcast.10), custom_call_target="tpu_custom_call" | custom-call | tf_op jit(solution)/shard_map/slice/pallas_call | solution.py:216
  6.6 0.0 copy-start
  6.7 0.1 collective-permute-start.3
  6.7 1.0 %slice.7 = bf16[96,1024]{1,0:T(8,128)(2,1)S(1)} custom-call(bf16[4,96,1024]{2,1,0:T(8,128)(2,1)} %bitcast.11), custom_call_target="tpu_custom_call" | custom-call | tf_op jit(solution)/shard_map/slice/pallas_call | solution.py:216
  7.7 3.0 %collective-permute-start.4 = (bf16[96,1024]{1,0:T(8,128)(2,1)S(1)}, bf16[96,1024]{1,0:T(8,128)(2,1)S(1)}, u32[]{:S(2)}, u32[]{:S(2)}) collective-permute-start(bf16[96,1024]{1,0:T(8,128)(2,1)S(1)} %slice.7), channel_id=1, source_target_pairs={{0,3},{1,2},{2,1},{3,0},{4,6},{5,7},{6,5},{7,4},{8,11},{9,10},{10,... | collective-permute-start | bytes 589832 | tf_op jit(solution)/shard_map/ppermute | solution.py:81
  10.7 0.9 %slice.4.refs_0_ = bf16[96,1024]{1,0:T(8,128)(2,1)S(1)} custom-call(bf16[4,96,1024]{2,1,0:T(8,128)(2,1)} %bitcast.12), custom_call_target="tpu_custom_call" | custom-call | tf_op jit(solution)/shard_map/slice/pallas_call | solution.py:216
  11.7 0.0 collective-permute-done.2.refs_1_
  11.7 8.7 %collective-permute-done.3.refs_2_ = bf16[96,1024]{1,0:T(8,128)(2,1)S(1)} collective-permute-done((bf16[96,1024]{1,0:T(8,128)(2,1)S(1)}, bf16[96,1024]{1,0:T(8,128)(2,1)S(1)}, u32[]{:S(2)}, u32[]{:S(2)}) %collective-permute-start.3) | collective-permute-done | bytes 196640 | tf_op jit(solution)/shard_map/ppermute | solution.py:81
  20.4 2.6 %update.1.refs_3_ = bf16[384,1024]{1,0:T(8,128)(2,1)S(1)} custom-call(bf16[96,1024]{1,0:T(8,128)(2,1)S(1)} %slice.4.refs_0_, bf16[96,1024]{1,0:T(8,128)(2,1)S(1)} %collective-permute-done.2.refs_1_, bf16[96,1024]{1,0:T(8,128)(2,1)S(1)} %collective-permute-done.3.refs_2_, bf16[96,1024]{1,0:T(8,128)(2,1)S(1)} %collective-permute-done.4.refs_3_, ...), custom_call_target="tpu_custom_call" | custom-call | flops 1170210816 | bytes 2359296 | tf_op jit(solution)/shard_map/update/pallas_call | solution.py:250
  23.0 1.6 %collective-permute-start.5 = (bf16[384,1024]{1,0:T(8,128)(2,1)S(1)}, bf16[384,1024]{1,0:T(8,128)(2,1)S(1)}, u32[]{:S(2)}, u32[]{:S(2)}) collective-permute-start(bf16[384,1024]{1,0:T(8,128)(2,1)S(1)} %update.1.refs_3_), channel_id=1, source_target_pairs={{0,16},{4,20},{8,24},{12,28},{16,0},{20,4},{24,8},{28,12},{1,17},{... | collective-permute-start | bytes 2359304 | tf_op jit(solution)/shard_map/ppermute | solution.py:264
  24.6 0.7 %copy-done.2 = s32[1,256,1]{1,2,0:T(1,128)S(1)} copy-done((s32[1,256,1]{1,2,0:T(1,128)S(1)}, s32[1,256,1]{1,2,0:T(1,128)}, u32[]{:S(2)}) %copy-start.2) | copy-done | bytes 1048
  25.3 1.0 %pack.1 = (bf16[128,1024]{1,0:T(8,128)(2,1)S(1)}, bf16[128,1024]{1,0:T(8,128)(2,1)S(1)}, bf16[128,1024]{1,0:T(8,128)(2,1)S(1)}, bf16[128,512]{1,0:T(8,128)(2,1)S(1)}, bf16[128,512]{1,0:T(8,128)(2,1)S(1)}) custom-call(s32[1,256]{1,0:T(1,128)S(1)} %bitcast.8, bf16[256,1024]{1,0:T(8,128)(2,1)S(1)} %bitcast.7), custom_call_target="tpu_custom_call" | custom-call | flops 268435456 | bytes 1572864 | tf_op jit(solution)/shard_map/pack/pallas_call | solution.py:229
  26.3 3.5 %collective-permute-start = (bf16[128,1024]{1,0:T(8,128)(2,1)S(1)}, bf16[128,1024]{1,0:T(8,128)(2,1)S(1)}, u32[]{:S(2)}, u32[]{:S(2)}) collective-permute-start(bf16[128,1024]{1,0:T(8,128)(2,1)S(1)} %get-tuple-element.11), channel_id=1, source_target_pairs={{0,1},{1,0},{2,3},{3,2},{4,5},{5,4},{6,7},{7,6},{8,9},{9,8},{10,11... | collective-permute-start | bytes 786440 | tf_op jit(solution)/shard_map/ppermute | solution.py:81
  29.8 2.6 %collective-permute-start.1 = (bf16[128,1024]{1,0:T(8,128)(2,1)S(1)}, bf16[128,1024]{1,0:T(8,128)(2,1)S(1)}, u32[]{:S(2)}, u32[]{:S(2)}) collective-permute-start(bf16[128,1024]{1,0:T(8,128)(2,1)S(1)} %get-tuple-element.12), channel_id=1, source_target_pairs={{0,3},{1,2},{2,0},{3,1},{4,7},{5,6},{6,4},{7,5},{8,11},{9,10},{10,... | collective-permute-start | bytes 786440 | tf_op jit(solution)/shard_map/ppermute | solution.py:81
  32.4 0.3 collective-permute-start.7
  32.7 0.3 collective-permute-start.6
  33.0 6.9 %collective-permute-done.refs_1_ = bf16[128,1024]{1,0:T(8,128)(2,1)S(1)} collective-permute-done((bf16[128,1024]{1,0:T(8,128)(2,1)S(1)}, bf16[128,1024]{1,0:T(8,128)(2,1)S(1)}, u32[]{:S(2)}, u32[]{:S(2)}) %collective-permute-start) | collective-permute-done | bytes 262176 | tf_op jit(solution)/shard_map/ppermute | solution.py:81
  39.9 10.3 %collective-permute-done.1.refs_2_ = bf16[128,1024]{1,0:T(8,128)(2,1)S(1)} collective-permute-done((bf16[128,1024]{1,0:T(8,128)(2,1)S(1)}, bf16[128,1024]{1,0:T(8,128)(2,1)S(1)}, u32[]{:S(2)}, u32[]{:S(2)}) %collective-permute-start.1) | collective-permute-done | bytes 262176 | tf_op jit(solution)/shard_map/ppermute | solution.py:81
  50.2 1.4 %project.1 = (bf16[384,1024]{1,0:T(8,128)(2,1)}, bf16[512,384]{1,0:T(8,128)(2,1)}, bf16[1024,384]{1,0:T(8,128)(2,1)S(1)}) custom-call(bf16[128,1024]{1,0:T(8,128)(2,1)S(1)} %get-tuple-element.10.refs_0_, bf16[128,1024]{1,0:T(8,128)(2,1)S(1)} %collective-permute-done.refs_1_, bf16[128,1024]{1,0:T(8,128)(2,1)S(1)} %collective-permute-done.1.refs_2_, ...), custom_call_target="tpu_custom_call" | custom-call | flops 301989888 | bytes 3440640 | tf_op jit(solution)/shard_map/project/pallas_call | solution.py:271
  51.5 0.0 collective-permute-done.7.block_ref
  51.5 0.2 part.1.part_ref
  51.8 0.9 %last.1 = bf16[512,384]{1,0:T(8,128)(2,1)} custom-call(bf16[128,512]{1,0:T(8,128)(2,1)S(1)} %collective-permute-done.6.block_ref, bf16[1024,384]{1,0:T(8,128)(2,1)S(1)} %get-tuple-element.15.turned_ref, f32[128,384]{1,0:T(8,128)S(1)} %part.1.part_ref, bf16[512,384]{1,0:T(8,128)(2,1)} %get-tuple-element.17._), custom_call_target="tpu_custom_call", output_to_operand_aliasing={{}: (3, {})} | custom-call | flops 100663296 | bytes 360448 | tf_op jit(solution)/shard_map/last/pallas_call | solution.py:307
  (7 shorter events, 0.0 us)
Async XLA Ops:
  1.6 10.1 %collective-permute-start.2 = (bf16[96,1024]{1,0:T(8,128)(2,1)S(1)}, bf16[96,1024]{1,0:T(8,128)(2,1)S(1)}, u32[]{:S(2)}, u32[]{:S(2)}) collective-permute-start(bf16[96,1024]{1,0:T(8,128)(2,1)S(1)} %slice.5), channel_id=1, source_target_pairs={{0,2},{1,0},{2,3},{3,1},{4,7},{5,6},{6,4},{7,5},{8,10},{9,8},{10,1... | collective-permute-start | bytes 589832 | tf_op jit(solution)/shard_map/ppermute | solution.py:81
  6.6 13.8 %copy-start = (bf16[1,1,384,1024]{3,2,1,0:T(8,128)(2,1)S(1)}, bf16[1,1,384,1024]{3,2,1,0:T(8,128)(2,1)}, u32[]{:S(2)}) copy-start(bf16[1,1,384,1024]{3,2,1,0:T(8,128)(2,1)} %param.5) | copy-start | bytes 2359300
  6.7 13.8 %collective-permute-start.3 = (bf16[96,1024]{1,0:T(8,128)(2,1)S(1)}, bf16[96,1024]{1,0:T(8,128)(2,1)S(1)}, u32[]{:S(2)}, u32[]{:S(2)}) collective-permute-start(bf16[96,1024]{1,0:T(8,128)(2,1)S(1)} %slice.6), channel_id=1, source_target_pairs={{0,1},{1,3},{2,0},{3,2},{4,5},{5,4},{6,7},{7,6},{8,9},{9,11},{10,8... | collective-permute-start | bytes 589832 | tf_op jit(solution)/shard_map/ppermute | solution.py:81
  7.7 12.7 %collective-permute-start.4 = (bf16[96,1024]{1,0:T(8,128)(2,1)S(1)}, bf16[96,1024]{1,0:T(8,128)(2,1)S(1)}, u32[]{:S(2)}, u32[]{:S(2)}) collective-permute-start(bf16[96,1024]{1,0:T(8,128)(2,1)S(1)} %slice.7), channel_id=1, source_target_pairs={{0,3},{1,2},{2,1},{3,0},{4,6},{5,7},{6,5},{7,4},{8,11},{9,10},{10,... | collective-permute-start | bytes 589832 | tf_op jit(solution)/shard_map/ppermute | solution.py:81
  20.4 4.2 %copy-start.1 = (bf16[1,256,1024]{2,1,0:T(8,128)(2,1)S(1)}, bf16[1,256,1024]{2,1,0:T(8,128)(2,1)}, u32[]{:S(2)}) copy-start(bf16[1,256,1024]{2,1,0:T(8,128)(2,1)} %param.6) | copy-start | bytes 1572868
  23.0 27.1 %collective-permute-start.5 = (bf16[384,1024]{1,0:T(8,128)(2,1)S(1)}, bf16[384,1024]{1,0:T(8,128)(2,1)S(1)}, u32[]{:S(2)}, u32[]{:S(2)}) collective-permute-start(bf16[384,1024]{1,0:T(8,128)(2,1)S(1)} %update.1.refs_3_), channel_id=1, source_target_pairs={{0,16},{4,20},{8,24},{12,28},{16,0},{20,4},{24,8},{28,12},{1,17},{... | collective-permute-start | bytes 2359304 | tf_op jit(solution)/shard_map/ppermute | solution.py:264
  24.6 0.7 %copy-start.2 = (s32[1,256,1]{1,2,0:T(1,128)S(1)}, s32[1,256,1]{1,2,0:T(1,128)}, u32[]{:S(2)}) copy-start(s32[1,256,1]{1,2,0:T(1,128)} %param.7) | copy-start | bytes 3076
  26.3 13.6 %collective-permute-start = (bf16[128,1024]{1,0:T(8,128)(2,1)S(1)}, bf16[128,1024]{1,0:T(8,128)(2,1)S(1)}, u32[]{:S(2)}, u32[]{:S(2)}) collective-permute-start(bf16[128,1024]{1,0:T(8,128)(2,1)S(1)} %get-tuple-element.11), channel_id=1, source_target_pairs={{0,1},{1,0},{2,3},{3,2},{4,5},{5,4},{6,7},{7,6},{8,9},{9,8},{10,11... | collective-permute-start | bytes 786440 | tf_op jit(solution)/shard_map/ppermute | solution.py:81
  29.8 20.3 %collective-permute-start.1 = (bf16[128,1024]{1,0:T(8,128)(2,1)S(1)}, bf16[128,1024]{1,0:T(8,128)(2,1)S(1)}, u32[]{:S(2)}, u32[]{:S(2)}) collective-permute-start(bf16[128,1024]{1,0:T(8,128)(2,1)S(1)} %get-tuple-element.12), channel_id=1, source_target_pairs={{0,3},{1,2},{2,0},{3,1},{4,7},{5,6},{6,4},{7,5},{8,11},{9,10},{10,... | collective-permute-start | bytes 786440 | tf_op jit(solution)/shard_map/ppermute | solution.py:81
  32.4 19.1 %collective-permute-start.7 = (bf16[128,512]{1,0:T(8,128)(2,1)S(1)}, bf16[128,512]{1,0:T(8,128)(2,1)S(1)}, u32[]{:S(2)}, u32[]{:S(2)}) collective-permute-start(bf16[128,512]{1,0:T(8,128)(2,1)S(1)} %get-tuple-element.16), channel_id=1, source_target_pairs={{0,2},{1,3},{2,1},{3,0},{4,6},{5,7},{6,5},{7,4},{8,10},{9,11},{10,... | collective-permute-start | bytes 393224 | tf_op jit(solution)/shard_map/ppermute | solution.py:81
  32.7 19.0 %collective-permute-start.6 = (bf16[128,512]{1,0:T(8,128)(2,1)S(1)}, bf16[128,512]{1,0:T(8,128)(2,1)S(1)}, u32[]{:S(2)}, u32[]{:S(2)}) collective-permute-start(bf16[128,512]{1,0:T(8,128)(2,1)S(1)} %get-tuple-element.14), channel_id=1, source_target_pairs={{0,2},{1,3},{2,1},{3,0},{4,6},{5,7},{6,5},{7,4},{8,10},{9,11},{10,... | collective-permute-start | bytes 393224 | tf_op jit(solution)/shard_map/ppermute | solution.py:81

commit v6 on v5

--- a/solution.py
+++ b/solution.py
@@ -155,49 +155,46 @@
         ).astype(jnp.bfloat16)
 
 
-def project_kernel(come, width, *refs):
-    nodes = len(come)
+def project_kernel(nodes, width, *refs):
     blocks, own_ref, partner_ref = refs[:nodes], *refs[nodes : nodes + 2]
-    weight_out, rows_out, turned_ref, weight_ref, slot_ref, rows_ref, sems = refs[nodes + 2 :]
-    me = lax.axis_index("fsdp")
+    weight_out, rows_ref, turned_ref, weight_ref, slot_ref, sem = refs[nodes + 2 :]
     capacity = blocks[0].shape[0]
     weight = (
         0.5 * (own_ref[...].astype(jnp.float32) + partner_ref[...].astype(jnp.float32))
     ).astype(jnp.bfloat16)
     weight_ref[...] = weight
-    copies = [pltpu.make_async_copy(weight_ref, weight_out, sems.at[nodes])]
-    copies[0].start()
+    cp = pltpu.make_async_copy(weight_ref, weight_out, sem)
+    cp.start()
     for k in range(nodes):
         slot_ref[k * capacity : (k + 1) * capacity, :] = blocks[k][...]
     rows_ref[...] = (dot_t(slot_ref[...], weight) * (1.0 / math.sqrt(width))).astype(jnp.bfloat16)
-    for k in range(nodes):
+    turned_ref[...] = weight.T
+    cp.wait()
+
+
+def part_kernel(block_ref, turned_ref, part_ref):
+    part_ref[...] = dot(block_ref[...], turned_ref[: block_ref.shape[1], :])
+
+
+def last_kernel(come, width, block_ref, turned_ref, part_ref, held_ref, rows_out, rows_ref, sems):
+    me = lax.axis_index("fsdp")
+    capacity = block_ref.shape[0]
+    early = len(come) - 1
+
+    def put(source, k):
         home = pl.ds(pl.multiple_of(at(come[k], me) * capacity, capacity), capacity)
-        copies.append(
-            pltpu.make_async_copy(
-                rows_ref.at[k * capacity : (k + 1) * capacity], rows_out.at[home], sems.at[k]
-            )
-        )
-        copies[-1].start()
-    turned_ref[...] = weight.T
+        cp = pltpu.make_async_copy(source, rows_out.at[home], sems.at[k])
+        cp.start()
+        return cp
+
+    copies = [put(held_ref.at[k * capacity : (k + 1) * capacity], k) for k in range(early)]
+    total = part_ref[...] + dot(
+        block_ref[...], turned_ref[turned_ref.shape[0] - block_ref.shape[1] :, :]
+    )
+    rows_ref[...] = (total * (1.0 / math.sqrt(width))).astype(jnp.bfloat16)
+    copies.append(put(rows_ref, early))
     for cp in copies:
         cp.wait()
-
-
-def part_kernel(block_ref, turned_ref, part_ref):
-    part_ref[...] = dot(block_ref[...], turned_ref[: block_ref.shape[1], :])
-
-
-def last_kernel(come, width, block_ref, turned_ref, part_ref, _, rows_out, rows_ref, sem):
-    me = lax.axis_index("fsdp")
-    capacity = block_ref.shape[0]
-    total = part_ref[...] + dot(
-        block_ref[...], turned_ref[turned_ref.shape[0] - block_ref.shape[1] :, :]
-    )
-    rows_ref[...] = (total * (1.0 / math.sqrt(width))).astype(jnp.bfloat16)
-    home = pl.ds(pl.multiple_of(at(come, me) * capacity, capacity), capacity)
-    cp = pltpu.make_async_copy(rows_ref, rows_out.at[home], sem)
-    cp.start()
-    cp.wait()
 
 
 def per_device(momentum, weights, tokens, routes):
@@ -268,20 +265,19 @@
     early = nodes - 1
     rows_shape = jax.ShapeDtypeStruct((nodes * capacity, total), jnp.bfloat16)
     hbm = pl.BlockSpec(memory_space=pltpu.HBM)
-    averaged, expert_rows, turned = pl.pallas_call(
-        functools.partial(project_kernel, come[:early], width),
+    averaged, held_rows, turned = pl.pallas_call(
+        functools.partial(project_kernel, early, width),
         out_shape=(
             jax.ShapeDtypeStruct((total, width), jnp.bfloat16),
-            rows_shape,
+            jax.ShapeDtypeStruct((early * capacity, total), jnp.bfloat16),
             jax.ShapeDtypeStruct((width, total), jnp.bfloat16),
         ),
         in_specs=[VMEM] * (early + 2),
-        out_specs=(hbm, hbm, VMEM),
+        out_specs=(hbm, VMEM, VMEM),
         scratch_shapes=[
             pltpu.VMEM((total, width), jnp.bfloat16),
             pltpu.VMEM((early * capacity, width), jnp.bfloat16),
-            pltpu.VMEM((early * capacity, total), jnp.bfloat16),
-            pltpu.SemaphoreType.DMA((nodes,)),
+            pltpu.SemaphoreType.DMA,
         ],
         compiler_params=pltpu.CompilerParams(vmem_limit_bytes=24 << 20),
         cost_estimate=pl.CostEstimate(
@@ -305,15 +301,14 @@
         name="part",
     )(slots[early], turned)
     expert_rows = pl.pallas_call(
-        functools.partial(last_kernel, come[early], width),
+        functools.partial(last_kernel, come, width),
         out_shape=rows_shape,
-        in_specs=[VMEM, VMEM, VMEM, hbm],
+        in_specs=[VMEM] * 4,
         out_specs=hbm,
         scratch_shapes=[
             pltpu.VMEM((capacity, total), jnp.bfloat16),
-            pltpu.SemaphoreType.DMA,
+            pltpu.SemaphoreType.DMA((nodes,)),
         ],
-        input_output_aliases={3: 0},
         compiler_params=pltpu.CompilerParams(vmem_limit_bytes=24 << 20),
         cost_estimate=pl.CostEstimate(
             flops=2 * capacity * width * total,
@@ -321,7 +316,7 @@
             transcendentals=0,
         ),
         name="last",
-    )(slots[early + 1], turned, part, expert_rows)
+    )(slots[early + 1], turned, part, held_rows)
     return (averaged[None, None], expert_rows[None, None])
 
 

time: 52.9 us -> 52.8 us (level)
  no operation moved by 1% of the time
where the time goes in v6:
time: 52.8 us; the launch traced here: 52.5 us
  waiting for transfers between devices  25.8 us (49%)
  starting transfers between devices  15.5 us (29%)
  Pallas kernels  9.8 us (19%)
  between operations  0.74 us (1%)
  local copies, waits for them, and re-layouts  0.69 us (1%)
    ppermute x7, waiting for transfers between devices, trade(): return lax.ppermute(block, ('replica', 'fsdp'), pairs)  25.8 us
    ppermute x7, starting transfers between devices, trade(): return lax.ppermute(block, ('replica', 'fsdp'), pairs)  13.9 us
    pallas_call x4, Pallas kernels, per_device(): pl.pallas_call(functools.partial(slice_kernel, step), out_shape=jax.Shape...  3.83 us
    pallas_call x1, Pallas kernels, per_device(): pl.pallas_call(functools.partial(update_kernel, [inverse(s) for s in far]...  2.62 us
    ppermute x1, starting transfers between devices, per_device(): lax.ppermute(updated, 'replica', [(i, i ^ 1 << GOSSIP_BIT) for i in range...  1.58 us
    pallas_call x1, Pallas kernels, per_device(): pl.pallas_call(functools.partial(project_kernel, early, width), out_shape...  1.22 us
  transfers between devices with their start and end apart: 8, of which 3 were waited for; matrix products, arithmetic and copies ran while one was open for 0% of the time, Pallas kernels for 10%

profile of v6, /device:TPU:0, one launch (start us, length us, event | category | flops | bytes accessed | tf_op | source)
XLA Modules:
  0.0 52.5 jit_solution(2666897922506807161)
XLA Ops:
  0.6 1.0 %slice.5 = bf16[96,1024]{1,0:T(8,128)(2,1)S(1)} custom-call(bf16[4,96,1024]{2,1,0:T(8,128)(2,1)} %bitcast.9), custom_call_target="tpu_custom_call" | custom-call | tf_op jit(solution)/shard_map/slice/pallas_call | solution.py:213
  1.6 4.1 %collective-permute-start.2 = (bf16[96,1024]{1,0:T(8,128)(2,1)S(1)}, bf16[96,1024]{1,0:T(8,128)(2,1)S(1)}, u32[]{:S(2)}, u32[]{:S(2)}) collective-permute-start(bf16[96,1024]{1,0:T(8,128)(2,1)S(1)} %slice.5), channel_id=1, source_target_pairs={{0,2},{1,0},{2,3},{3,1},{4,7},{5,6},{6,4},{7,5},{8,10},{9,8},{10,1... | collective-permute-start | bytes 589832 | tf_op jit(solution)/shard_map/ppermute | solution.py:81
  5.7 0.9 %slice.6 = bf16[96,1024]{1,0:T(8,128)(2,1)S(1)} custom-call(bf16[4,96,1024]{2,1,0:T(8,128)(2,1)} %bitcast.10), custom_call_target="tpu_custom_call" | custom-call | tf_op jit(solution)/shard_map/slice/pallas_call | solution.py:213
  6.6 0.0 copy-start
  6.7 0.1 collective-permute-start.3
  6.7 1.0 %slice.7 = bf16[96,1024]{1,0:T(8,128)(2,1)S(1)} custom-call(bf16[4,96,1024]{2,1,0:T(8,128)(2,1)} %bitcast.11), custom_call_target="tpu_custom_call" | custom-call | tf_op jit(solution)/shard_map/slice/pallas_call | solution.py:213
  7.7 3.0 %collective-permute-start.4 = (bf16[96,1024]{1,0:T(8,128)(2,1)S(1)}, bf16[96,1024]{1,0:T(8,128)(2,1)S(1)}, u32[]{:S(2)}, u32[]{:S(2)}) collective-permute-start(bf16[96,1024]{1,0:T(8,128)(2,1)S(1)} %slice.7), channel_id=1, source_target_pairs={{0,3},{1,2},{2,1},{3,0},{4,6},{5,7},{6,5},{7,4},{8,11},{9,10},{10,... | collective-permute-start | bytes 589832 | tf_op jit(solution)/shard_map/ppermute | solution.py:81
  10.7 0.9 %slice.4.refs_0_ = bf16[96,1024]{1,0:T(8,128)(2,1)S(1)} custom-call(bf16[4,96,1024]{2,1,0:T(8,128)(2,1)} %bitcast.12), custom_call_target="tpu_custom_call" | custom-call | tf_op jit(solution)/shard_map/slice/pallas_call | solution.py:213
  11.7 8.7 %collective-permute-done.3.refs_2_ = bf16[96,1024]{1,0:T(8,128)(2,1)S(1)} collective-permute-done((bf16[96,1024]{1,0:T(8,128)(2,1)S(1)}, bf16[96,1024]{1,0:T(8,128)(2,1)S(1)}, u32[]{:S(2)}, u32[]{:S(2)}) %collective-permute-start.3) | collective-permute-done | bytes 196640 | tf_op jit(solution)/shard_map/ppermute | solution.py:81
  20.4 2.6 %update.1.refs_3_ = bf16[384,1024]{1,0:T(8,128)(2,1)S(1)} custom-call(bf16[96,1024]{1,0:T(8,128)(2,1)S(1)} %slice.4.refs_0_, bf16[96,1024]{1,0:T(8,128)(2,1)S(1)} %collective-permute-done.2.refs_1_, bf16[96,1024]{1,0:T(8,128)(2,1)S(1)} %collective-permute-done.3.refs_2_, bf16[96,1024]{1,0:T(8,128)(2,1)S(1)} %collective-permute-done.4.refs_3_, ...), custom_call_target="tpu_custom_call" | custom-call | flops 1170210816 | bytes 2359296 | tf_op jit(solution)/shard_map/update/pallas_call | solution.py:247
  23.0 1.6 %collective-permute-start.5 = (bf16[384,1024]{1,0:T(8,128)(2,1)S(1)}, bf16[384,1024]{1,0:T(8,128)(2,1)S(1)}, u32[]{:S(2)}, u32[]{:S(2)}) collective-permute-start(bf16[384,1024]{1,0:T(8,128)(2,1)S(1)} %update.1.refs_3_), channel_id=1, source_target_pairs={{0,16},{4,20},{8,24},{12,28},{16,0},{20,4},{24,8},{28,12},{1,17},{... | collective-permute-start | bytes 2359304 | tf_op jit(solution)/shard_map/ppermute | solution.py:261
  24.6 0.7 %copy-done.2 = s32[1,256,1]{1,2,0:T(1,128)S(1)} copy-done((s32[1,256,1]{1,2,0:T(1,128)S(1)}, s32[1,256,1]{1,2,0:T(1,128)}, u32[]{:S(2)}) %copy-start.2) | copy-done | bytes 1048
  25.3 1.0 %pack.1 = (bf16[128,1024]{1,0:T(8,128)(2,1)S(1)}, bf16[128,1024]{1,0:T(8,128)(2,1)S(1)}, bf16[128,1024]{1,0:T(8,128)(2,1)S(1)}, bf16[128,512]{1,0:T(8,128)(2,1)S(1)}, bf16[128,512]{1,0:T(8,128)(2,1)S(1)}) custom-call(s32[1,256]{1,0:T(1,128)S(1)} %bitcast.8, bf16[256,1024]{1,0:T(8,128)(2,1)S(1)} %bitcast.7), custom_call_target="tpu_custom_call" | custom-call | flops 268435456 | bytes 1572864 | tf_op jit(solution)/shard_map/pack/pallas_call | solution.py:226
  26.3 3.5 %collective-permute-start = (bf16[128,1024]{1,0:T(8,128)(2,1)S(1)}, bf16[128,1024]{1,0:T(8,128)(2,1)S(1)}, u32[]{:S(2)}, u32[]{:S(2)}) collective-permute-start(bf16[128,1024]{1,0:T(8,128)(2,1)S(1)} %get-tuple-element.11), channel_id=1, source_target_pairs={{0,1},{1,0},{2,3},{3,2},{4,5},{5,4},{6,7},{7,6},{8,9},{9,8},{10,11... | collective-permute-start | bytes 786440 | tf_op jit(solution)/shard_map/ppermute | solution.py:81
  29.8 2.6 %collective-permute-start.1 = (bf16[128,1024]{1,0:T(8,128)(2,1)S(1)}, bf16[128,1024]{1,0:T(8,128)(2,1)S(1)}, u32[]{:S(2)}, u32[]{:S(2)}) collective-permute-start(bf16[128,1024]{1,0:T(8,128)(2,1)S(1)} %get-tuple-element.12), channel_id=1, source_target_pairs={{0,3},{1,2},{2,0},{3,1},{4,7},{5,6},{6,4},{7,5},{8,11},{9,10},{10,... | collective-permute-start | bytes 786440 | tf_op jit(solution)/shard_map/ppermute | solution.py:81
  32.4 0.3 collective-permute-start.7
  32.7 0.3 collective-permute-start.6
  33.0 6.9 %collective-permute-done.refs_1_ = bf16[128,1024]{1,0:T(8,128)(2,1)S(1)} collective-permute-done((bf16[128,1024]{1,0:T(8,128)(2,1)S(1)}, bf16[128,1024]{1,0:T(8,128)(2,1)S(1)}, u32[]{:S(2)}, u32[]{:S(2)}) %collective-permute-start) | collective-permute-done | bytes 262176 | tf_op jit(solution)/shard_map/ppermute | solution.py:81
  39.9 10.3 %collective-permute-done.1.refs_2_ = bf16[128,1024]{1,0:T(8,128)(2,1)S(1)} collective-permute-done((bf16[128,1024]{1,0:T(8,128)(2,1)S(1)}, bf16[128,1024]{1,0:T(8,128)(2,1)S(1)}, u32[]{:S(2)}, u32[]{:S(2)}) %collective-permute-start.1) | collective-permute-done | bytes 262176 | tf_op jit(solution)/shard_map/ppermute | solution.py:81
  50.2 1.2 %project.1 = (bf16[384,1024]{1,0:T(8,128)(2,1)}, bf16[384,384]{1,0:T(8,128)(2,1)S(1)}, bf16[1024,384]{1,0:T(8,128)(2,1)S(1)}) custom-call(bf16[128,1024]{1,0:T(8,128)(2,1)S(1)} %get-tuple-element.10.refs_0_, bf16[128,1024]{1,0:T(8,128)(2,1)S(1)} %collective-permute-done.refs_1_, bf16[128,1024]{1,0:T(8,128)(2,1)S(1)} %collective-permute-done.1.refs_2_, ...), custom_call_target="tpu_custom_call" | custom-call | flops 301989888 | bytes 3440640 | tf_op jit(solution)/shard_map/project/pallas_call | solution.py:268
  51.4 0.0 collective-permute-done.7.block_ref
  51.4 0.2 part.1.part_ref
  51.6 0.0 collective-permute-done.6.block_ref
  51.6 0.9 %last.1 = bf16[512,384]{1,0:T(8,128)(2,1)} custom-call(bf16[128,512]{1,0:T(8,128)(2,1)S(1)} %collective-permute-done.6.block_ref, bf16[1024,384]{1,0:T(8,128)(2,1)S(1)} %get-tuple-element.15.turned_ref, f32[128,384]{1,0:T(8,128)S(1)} %part.1.part_ref, bf16[384,384]{1,0:T(8,128)(2,1)S(1)} %get-tuple-element.17.held_ref), custom_call_target="tpu_custom_call" | custom-call | flops 100663296 | bytes 360448 | tf_op jit(solution)/shard_map/last/pallas_call | solution.py:303
  (7 shorter events, 0.0 us)
Async XLA Ops:
  1.6 10.1 %collective-permute-start.2 = (bf16[96,1024]{1,0:T(8,128)(2,1)S(1)}, bf16[96,1024]{1,0:T(8,128)(2,1)S(1)}, u32[]{:S(2)}, u32[]{:S(2)}) collective-permute-start(bf16[96,1024]{1,0:T(8,128)(2,1)S(1)} %slice.5), channel_id=1, source_target_pairs={{0,2},{1,0},{2,3},{3,1},{4,7},{5,6},{6,4},{7,5},{8,10},{9,8},{10,1... | collective-permute-start | bytes 589832 | tf_op jit(solution)/shard_map/ppermute | solution.py:81
  6.6 13.8 %copy-start = (bf16[1,1,384,1024]{3,2,1,0:T(8,128)(2,1)S(1)}, bf16[1,1,384,1024]{3,2,1,0:T(8,128)(2,1)}, u32[]{:S(2)}) copy-start(bf16[1,1,384,1024]{3,2,1,0:T(8,128)(2,1)} %param.5) | copy-start | bytes 2359300
  6.7 13.8 %collective-permute-start.3 = (bf16[96,1024]{1,0:T(8,128)(2,1)S(1)}, bf16[96,1024]{1,0:T(8,128)(2,1)S(1)}, u32[]{:S(2)}, u32[]{:S(2)}) collective-permute-start(bf16[96,1024]{1,0:T(8,128)(2,1)S(1)} %slice.6), channel_id=1, source_target_pairs={{0,1},{1,3},{2,0},{3,2},{4,5},{5,4},{6,7},{7,6},{8,9},{9,11},{10,8... | collective-permute-start | bytes 589832 | tf_op jit(solution)/shard_map/ppermute | solution.py:81
  7.7 12.7 %collective-permute-start.4 = (bf16[96,1024]{1,0:T(8,128)(2,1)S(1)}, bf16[96,1024]{1,0:T(8,128)(2,1)S(1)}, u32[]{:S(2)}, u32[]{:S(2)}) collective-permute-start(bf16[96,1024]{1,0:T(8,128)(2,1)S(1)} %slice.7), channel_id=1, source_target_pairs={{0,3},{1,2},{2,1},{3,0},{4,6},{5,7},{6,5},{7,4},{8,11},{9,10},{10,... | collective-permute-start | bytes 589832 | tf_op jit(solution)/shard_map/ppermute | solution.py:81
  20.4 4.2 %copy-start.1 = (bf16[1,256,1024]{2,1,0:T(8,128)(2,1)S(1)}, bf16[1,256,1024]{2,1,0:T(8,128)(2,1)}, u32[]{:S(2)}) copy-start(bf16[1,256,1024]{2,1,0:T(8,128)(2,1)} %param.6) | copy-start | bytes 1572868
  23.0 27.1 %collective-permute-start.5 = (bf16[384,1024]{1,0:T(8,128)(2,1)S(1)}, bf16[384,1024]{1,0:T(8,128)(2,1)S(1)}, u32[]{:S(2)}, u32[]{:S(2)}) collective-permute-start(bf16[384,1024]{1,0:T(8,128)(2,1)S(1)} %update.1.refs_3_), channel_id=1, source_target_pairs={{0,16},{4,20},{8,24},{12,28},{16,0},{20,4},{24,8},{28,12},{1,17},{... | collective-permute-start | bytes 2359304 | tf_op jit(solution)/shard_map/ppermute | solution.py:261
  24.6 0.7 %copy-start.2 = (s32[1,256,1]{1,2,0:T(1,128)S(1)}, s32[1,256,1]{1,2,0:T(1,128)}, u32[]{:S(2)}) copy-start(s32[1,256,1]{1,2,0:T(1,128)} %param.7) | copy-start | bytes 3076
  26.3 13.6 %collective-permute-start = (bf16[128,1024]{1,0:T(8,128)(2,1)S(1)}, bf16[128,1024]{1,0:T(8,128)(2,1)S(1)}, u32[]{:S(2)}, u32[]{:S(2)}) collective-permute-start(bf16[128,1024]{1,0:T(8,128)(2,1)S(1)} %get-tuple-element.11), channel_id=1, source_target_pairs={{0,1},{1,0},{2,3},{3,2},{4,5},{5,4},{6,7},{7,6},{8,9},{9,8},{10,11... | collective-permute-start | bytes 786440 | tf_op jit(solution)/shard_map/ppermute | solution.py:81
  29.8 20.3 %collective-permute-start.1 = (bf16[128,1024]{1,0:T(8,128)(2,1)S(1)}, bf16[128,1024]{1,0:T(8,128)(2,1)S(1)}, u32[]{:S(2)}, u32[]{:S(2)}) collective-permute-start(bf16[128,1024]{1,0:T(8,128)(2,1)S(1)} %get-tuple-element.12), channel_id=1, source_target_pairs={{0,3},{1,2},{2,0},{3,1},{4,7},{5,6},{6,4},{7,5},{8,11},{9,10},{10,... | collective-permute-start | bytes 786440 | tf_op jit(solution)/shard_map/ppermute | solution.py:81
  32.4 19.0 %collective-permute-start.7 = (bf16[128,512]{1,0:T(8,128)(2,1)S(1)}, bf16[128,512]{1,0:T(8,128)(2,1)S(1)}, u32[]{:S(2)}, u32[]{:S(2)}) collective-permute-start(bf16[128,512]{1,0:T(8,128)(2,1)S(1)} %get-tuple-element.16), channel_id=1, source_target_pairs={{0,2},{1,3},{2,1},{3,0},{4,6},{5,7},{6,5},{7,4},{8,10},{9,11},{10,... | collective-permute-start | bytes 393224 | tf_op jit(solution)/shard_map/ppermute | solution.py:81
  32.7 18.9 %collective-permute-start.6 = (bf16[128,512]{1,0:T(8,128)(2,1)S(1)}, bf16[128,512]{1,0:T(8,128)(2,1)S(1)}, u32[]{:S(2)}, u32[]{:S(2)}) collective-permute-start(bf16[128,512]{1,0:T(8,128)(2,1)S(1)} %get-tuple-element.14), channel_id=1, source_target_pairs={{0,2},{1,3},{2,1},{3,0},{4,6},{5,7},{6,5},{7,4},{8,10},{9,11},{10,... | collective-permute-start | bytes 393224 | tf_op jit(solution)/shard_map/ppermute | solution.py:81
